TPU v7x, 32 devices: a whole 2x2x4 slice. The times are simulated.
32 devices in a mesh: geo: 8 (over z, y), rep: 4 (over x, core).
Axes of the slice: x: 2, y: 2, z: 4, core: 2. Of those that a mesh axis runs over, the one named last changes fastest.
Arguments:
- base: float32 [65536], P(('geo', 'rep')), may hold values from 0.5 to 2
- job_res: int32 [65536], P(('geo', 'rep')), may hold values from 0 to 255
- job_slot: int32 [65536], P(('geo', 'rep')), may hold values from 0 to 255
- job_cell: int32 [65536], P(('geo', 'rep')), may hold values from 0 to 29
- needed: int32 [8, 8, 1], P('geo'), may hold values from 0 to 7
- lam_res: float32 [30, 2048], P(None, 'geo'), may hold values from -2 to 2
- lam_work: float32 [30, 2048], P(None, 'geo'), may hold values from -2 to 2
- target_res: float32 [30, 2048], P(None, 'geo'), may hold values from 0.3 to 3
- target_work: float32 [30, 2048], P(None, 'geo'), may hold values from 0.3 to 3
Outputs:
- step_res: float32 [30, 2048], P(None, 'geo')
- step_work: float32 [30, 2048], P(None, 'geo')
- resid_res: float32 [30, 2048], P(None, 'geo')
- resid_work: float32 [30, 2048], P(None, 'geo')
Inputs may be any that keep to these rules, and one draw needn't show every extreme that they name: needed[g, p, k] is a block of owner p's tracts; block b covers that owner's local tracts b * 32 to b * 32 + 31.
All inputs are finite; a program needn't handle non-finite values.
Results may differ from a plain program's by a relative error of at most 0.0003.
Values sent between devices are 32-bit elements; how exact they have to be, the bound alone decides.
No kernel may reach another device: no remote copies, remote signals or barrier semaphores. Data moves between devices by JAX's collectives and lax.ppermute only.
A program may use at most 64 MiB of HBM per device.

v0:
```python
import jax
import jax.numpy as jnp
from jax import lax
from jax.sharding import PartitionSpec as P

BLK = 32
ITERS = 3


RIDGE = 0.5


def body(base, job_res, job_slot, job_cell, needed, lam_res, lam_work, target_res, target_work):
    cells, tracts_dev = lam_res.shape
    blocks_dev = tracts_dev // BLK
    requests = lax.all_to_all(needed[0], "geo", split_axis=0, concat_axis=0, tiled=True)
    sources, listed = requests.shape
    onehot = (
        requests[:, :, None] == jnp.arange(blocks_dev, dtype=jnp.int32)[None, None, :]
    ).astype(jnp.float32)
    slot_shape = (sources, listed, cells, BLK)
    slot_count = sources * listed * cells * BLK
    res_index = job_cell * tracts_dev + job_res
    work_index = (job_slot // BLK * cells + job_cell) * BLK + job_slot % BLK

    def serve(table):
        blocks = table.reshape(cells, blocks_dev, BLK).transpose(1, 0, 2)
        return jnp.take(blocks, requests, axis=0)

    def pick(fetched):
        return fetched.reshape(-1)[work_index]

    def fold(arrived):
        return jnp.einsum("skb,skcx->cbx", onehot, arrived, precision=lax.Precision.HIGHEST)

    def totals(values):
        res_part = jax.ops.segment_sum(values, res_index, num_segments=cells * tracts_dev).reshape(
            cells, tracts_dev
        )
        work_part = jax.ops.segment_sum(values, work_index, num_segments=slot_count).reshape(
            slot_shape
        )
        arrived = lax.all_to_all(work_part, "geo", split_axis=0, concat_axis=0, tiled=True)
        folded = fold(arrived)
        return lax.psum((res_part, folded.reshape(cells, tracts_dev)), "rep")

    def squares(part_res, part_work):
        local = jnp.sum(part_res * part_res) + jnp.sum(part_work * part_work)
        return lax.psum(local, "geo")

    fetched_lam = lax.all_to_all(serve(lam_work), "geo", split_axis=0, concat_axis=0, tiled=True)
    weight = base * jnp.exp(lam_res.reshape(-1)[res_index] + pick(fetched_lam))
    total_res, total_work = totals(weight)
    resid_res = -(total_res - target_res)
    resid_work = -(total_work - target_work)
    step_res = jnp.zeros_like(resid_res)
    step_work = jnp.zeros_like(resid_work)
    dir_res, dir_work = (resid_res, resid_work)
    norm_now = squares(resid_res, resid_work)
    for turn in range(ITERS):
        served = serve(dir_work)
        dir_piece = lax.all_to_all(served, "geo", split_axis=0, concat_axis=0, tiled=True)
        along = dir_res.reshape(-1)[res_index] + pick(dir_piece)
        image_res, image_work = totals(weight * along)
        image_res = image_res + RIDGE * dir_res
        image_work = image_work + RIDGE * dir_work
        local_curv = jnp.sum(dir_res * image_res) + jnp.sum(dir_work * image_work)
        alpha = norm_now / lax.psum(local_curv, "geo")
        step_res = step_res + alpha * dir_res
        step_work = step_work + alpha * dir_work
        resid_res = resid_res - alpha * image_res
        resid_work = resid_work - alpha * image_work
        norm_next = squares(resid_res, resid_work)
        dir_res = resid_res + norm_next / norm_now * dir_res
        dir_work = resid_work + norm_next / norm_now * dir_work
        norm_now = norm_next
    return (step_res, step_work, resid_res, resid_work)


def solution(mesh):
    in_specs = (
        P(("geo", "rep")),
        P(("geo", "rep")),
        P(("geo", "rep")),
        P(("geo", "rep")),
        P("geo", None, None),
        P(None, "geo"),
        P(None, "geo"),
        P(None, "geo"),
        P(None, "geo"),
    )
    out_specs = (P(None, "geo"), P(None, "geo"), P(None, "geo"), P(None, "geo"))
    return jax.shard_map(body, mesh=mesh, in_specs=in_specs, out_specs=out_specs, check_vma=False)
```

profile of v0, /device:TPU:0, one launch (start us, length us, event | category | flops | bytes accessed | tf_op | source)
XLA Modules:
  0.0 438.6 jit_solution(15643490933301832814)
XLA Ops:
  2.0 7.3 %all-to-all-start = ((s32[8,1,1]{2,1,0:T(1,128)}), s32[8,1,1]{2,1,0:T(1,128)S(1)}, u32[]{:S(2)}, u32[]{:S(2)}) async-start(s32[8,1,1]{2,1,0:T(1,128)} %copy.79), calls=%async_computation | async-start | bytes 8192 | tf_op jit(solution)/shard_map/all_to_all | solution.py:16
  9.3 0.8 reshape.200
  10.2 5.5 %all-to-all-done = s32[8,1,1]{2,1,0:T(1,128)S(1)} async-done(((s32[8,1,1]{2,1,0:T(1,128)}), s32[8,1,1]{2,1,0:T(1,128)S(1)}, u32[]{:S(2)}, u32[]{:S(2)}) %all-to-all-start) | async-done | bytes 64 | tf_op jit(solution)/shard_map/all_to_all | solution.py:16
  17.3 0.9 reduce.10
  18.2 0.7 reshape.453
  19.0 3.5 all-to-all-start.1
  23.2 11.8 %gather_fusion = f32[2048]{0:T(1024)S(1)} fusion(f32[7680]{0:T(1024)S(1)} %reshape.199, s32[2048]{0:T(1024)S(1)} %get-tuple-element.31), kind=kCustom, calls=%fused_computation.4 | custom fusion | bytes 24576 | tf_op jit(solution)/shard_map/gather | solution.py:52
  36.4 11.8 %gather_fusion.1 = f32[2048]{0:T(1024)S(1)} fusion(f32[7680]{0:T(1024)S(1)} %reshape.201, s32[2048]{0:T(1024)S(1)} %get-tuple-element.19), kind=kCustom, calls=%fused_computation.5 | custom fusion | bytes 24576 | tf_op jit(solution)/shard_map/gather | solution.py:31
  48.2 11.3 %scatter_custom_fusion.1 = f32[7680]{0:T(1024)S(1)} fusion(s32[2048]{0:T(1024)S(1)} %get-tuple-element.20, f32[2048]{0:T(1024)S(1)} %exponential_multiply_fusion, f32[]{:T(128)} %constant.40.clone.1), kind=kCustom, calls=%fused_computation.84 | custom fusion | flops 2048 | bytes 30724 | tf_op jit(solution)/shard_map/scatter-add | solution.py:40
  59.7 0.9 reduce.12
  60.6 0.7 reshape.455
  61.4 5.9 %all-to-all-start.2 = ((f32[8,1,960]{2,1,0:T(1,128)}), f32[8,1,960]{2,1,0:T(1,128)S(1)}, u32[]{:S(2)}, u32[]{:S(2)}) async-start(f32[8,1,960]{2,1,0:T(1,128)} %reshape.455), calls=%async_computation.2 | async-start | bytes 65536 | tf_op jit(solution)/shard_map/all_to_all | solution.py:43
  67.3 11.3 %scatter_custom_fusion = f32[7680]{0:T(1024)S(1)} fusion(s32[2048]{0:T(1024)S(1)} %get-tuple-element.32, f32[2048]{0:T(1024)S(1)} %exponential_multiply_fusion, f32[]{:T(128)} %constant.40.clone.1), kind=kCustom, calls=%fused_computation.86 | custom fusion | flops 2048 | bytes 30724 | tf_op jit(solution)/shard_map/scatter-add | solution.py:37
  79.9 10.7 %all-reduce.4 = (f32[30,256]{1,0:T(8,128)S(1)}, f32[30,256]{1,0:T(8,128)S(1)}) all-reduce(f32[30,256]{1,0:T(8,128)S(1)} %reshape.202, f32[30,256]{1,0:T(8,128)S(1)} %reshape.205), channel_id=1, replica_groups=mesh['geo'=8,'rep'=4] {'rep'}, use_global_device_ids=true, to_apply=%region_1.3 | all-reduce | flops 15360 | bytes 122880 | tf_op jit(solution)/shard_map/psum | solution.py:45
  92.2 0.9 reduce.14
  93.1 0.7 reshape.457
  93.9 6.0 %all-to-all-start.3 = ((f32[8,1,960]{2,1,0:T(1,128)}), f32[8,1,960]{2,1,0:T(1,128)S(1)}, u32[]{:S(2)}, u32[]{:S(2)}) async-start(f32[8,1,960]{2,1,0:T(1,128)} %reshape.457), calls=%async_computation.3 | async-start | bytes 65536 | tf_op jit(solution)/shard_map/all_to_all | solution.py:62
  99.9 11.8 %gather_fusion.2 = f32[2048]{0:T(1024)S(1)} fusion(f32[7680]{0:T(1024)S(1)} %reshape.206, s32[2048]{0:T(1024)S(1)} %get-tuple-element.31), kind=kCustom, calls=%fused_computation.6 | custom fusion | bytes 24576 | tf_op jit(solution)/shard_map/gather | solution.py:63
  113.0 11.8 %gather_fusion.3 = f32[2048]{0:T(1024)S(1)} fusion(f32[7680]{0:T(1024)S(1)} %reshape.208, s32[2048]{0:T(1024)S(1)} %get-tuple-element.19), kind=kCustom, calls=%fused_computation.7 | custom fusion | bytes 24576 | tf_op jit(solution)/shard_map/gather | solution.py:31
  124.8 11.3 %scatter_custom_fusion.3 = f32[7680]{0:T(1024)S(1)} fusion(s32[2048]{0:T(1024)S(1)} %get-tuple-element.20, f32[2048]{0:T(1024)S(1)} %add_multiply_fusion.2, f32[]{:T(128)} %constant.40.clone.1), kind=kCustom, calls=%fused_computation.80 | custom fusion | flops 2048 | bytes 30724 | tf_op jit(solution)/shard_map/scatter-add | solution.py:40
  136.3 0.9 reduce.16
  137.3 0.7 reshape.459
  138.0 6.0 %all-to-all-start.4 = ((f32[8,1,960]{2,1,0:T(1,128)}), f32[8,1,960]{2,1,0:T(1,128)S(1)}, u32[]{:S(2)}, u32[]{:S(2)}) async-start(f32[8,1,960]{2,1,0:T(1,128)} %reshape.459), calls=%async_computation.4 | async-start | bytes 65536 | tf_op jit(solution)/shard_map/all_to_all | solution.py:43
  145.3 11.5 %scatter_custom_fusion.2 = f32[7680]{0:T(1024)S(1)} fusion(s32[2048]{0:T(1024)S(1)} %get-tuple-element.32, f32[2048]{0:T(1024)S(1)} %add_multiply_fusion.2, f32[]{:T(128)} %constant.40.clone.1), kind=kCustom, calls=%fused_computation.82 | custom fusion | flops 2048 | bytes 30724 | tf_op jit(solution)/shard_map/scatter-add | solution.py:37
  158.1 10.7 %all-reduce.3 = (f32[30,256]{1,0:T(8,128)S(1)}, f32[30,256]{1,0:T(8,128)S(1)}) all-reduce(f32[30,256]{1,0:T(8,128)S(1)} %reshape.209, f32[30,256]{1,0:T(8,128)S(1)} %reshape.212), channel_id=1, replica_groups=mesh['geo'=8,'rep'=4] {'rep'}, use_global_device_ids=true, to_apply=%region_8.10 | all-reduce | flops 15360 | bytes 122880 | tf_op jit(solution)/shard_map/psum | solution.py:45
  171.3 22.4 %all-reduce = (f32[]{:T(128)}, f32[]{:T(128)}) all-reduce(f32[]{:T(128)S(6)} %add.154, f32[]{:T(128)S(6)} %add.158), channel_id=1, replica_groups=mesh['geo'=8,'rep'=4] {'geo'}, use_global_device_ids=true, to_apply=%region_6.8 | all-reduce | flops 2 | bytes 16 | tf_op jit(solution)/shard_map/psum | solution.py:49
  197.5 17.7 %psum.104 = f32[]{:T(128)} all-reduce(f32[]{:T(128)S(6)} %add.159), channel_id=1, replica_groups=mesh['geo'=8,'rep'=4] {'geo'}, use_global_device_ids=true, to_apply=%region_16.18 | all-reduce | flops 1 | bytes 8 | tf_op jit(solution)/shard_map/psum | solution.py:49
  217.5 0.9 reduce.18
  219.2 3.3 all-to-all-start.5
  222.6 11.8 %gather_fusion.4 = f32[2048]{0:T(1024)S(1)} fusion(f32[7680]{0:T(1024)S(1)} %reshape.213, s32[2048]{0:T(1024)S(1)} %get-tuple-element.31), kind=kCustom, calls=%fused_computation.8 | custom fusion | bytes 24576 | tf_op jit(solution)/shard_map/gather | solution.py:63
  235.7 11.8 %gather_fusion.5 = f32[2048]{0:T(1024)S(1)} fusion(f32[7680]{0:T(1024)S(1)} %reshape.215, s32[2048]{0:T(1024)S(1)} %get-tuple-element.19), kind=kCustom, calls=%fused_computation.9 | custom fusion | bytes 24576 | tf_op jit(solution)/shard_map/gather | solution.py:31
  247.5 11.3 %scatter_custom_fusion.5 = f32[7680]{0:T(1024)S(1)} fusion(s32[2048]{0:T(1024)S(1)} %get-tuple-element.20, f32[2048]{0:T(1024)S(1)} %add_multiply_fusion.1, f32[]{:T(128)} %constant.40.clone.1), kind=kCustom, calls=%fused_computation.76 | custom fusion | flops 2048 | bytes 30724 | tf_op jit(solution)/shard_map/scatter-add | solution.py:40
  259.0 0.9 reduce.20
  260.7 5.9 %all-to-all-start.6 = ((f32[8,1,960]{2,1,0:T(1,128)}), f32[8,1,960]{2,1,0:T(1,128)S(1)}, u32[]{:S(2)}, u32[]{:S(2)}) async-start(f32[8,1,960]{2,1,0:T(1,128)} %reshape.463), calls=%async_computation.6 | async-start | bytes 65536 | tf_op jit(solution)/shard_map/all_to_all | solution.py:43
  266.6 11.3 %scatter_custom_fusion.4 = f32[7680]{0:T(1024)S(1)} fusion(s32[2048]{0:T(1024)S(1)} %get-tuple-element.32, f32[2048]{0:T(1024)S(1)} %add_multiply_fusion.1, f32[]{:T(128)} %constant.40.clone.1), kind=kCustom, calls=%fused_computation.78 | custom fusion | flops 2048 | bytes 30724 | tf_op jit(solution)/shard_map/scatter-add | solution.py:37
  279.2 10.7 %all-reduce.2 = (f32[30,256]{1,0:T(8,128)S(1)}, f32[30,256]{1,0:T(8,128)S(1)}) all-reduce(f32[30,256]{1,0:T(8,128)S(1)} %reshape.216, f32[30,256]{1,0:T(8,128)S(1)} %reshape.219), channel_id=1, replica_groups=mesh['geo'=8,'rep'=4] {'rep'}, use_global_device_ids=true, to_apply=%region_18.20 | all-reduce | flops 15360 | bytes 122880 | tf_op jit(solution)/shard_map/psum | solution.py:45
  292.4 22.3 %psum.107 = f32[]{:T(128)} all-reduce(f32[]{:T(128)S(6)} %add.165), channel_id=1, replica_groups=mesh['geo'=8,'rep'=4] {'geo'}, use_global_device_ids=true, to_apply=%region_23.25 | all-reduce | flops 1 | bytes 8 | tf_op jit(solution)/shard_map/psum | solution.py:68
  318.7 17.7 %psum.108 = f32[]{:T(128)} all-reduce(f32[]{:T(128)S(6)} %add.167), channel_id=1, replica_groups=mesh['geo'=8,'rep'=4] {'geo'}, use_global_device_ids=true, to_apply=%region_26.28 | all-reduce | flops 1 | bytes 8 | tf_op jit(solution)/shard_map/psum | solution.py:49
  338.6 0.9 reduce.22
  340.3 3.3 all-to-all-start.7
  343.7 11.8 %gather_fusion.6 = f32[2048]{0:T(1024)S(1)} fusion(f32[7680]{0:T(1024)S(1)} %reshape.220, s32[2048]{0:T(1024)S(1)} %get-tuple-element.31), kind=kCustom, calls=%fused_computation.10 | custom fusion | bytes 24576 | tf_op jit(solution)/shard_map/gather | solution.py:63
  356.8 11.8 %gather_fusion.7 = f32[2048]{0:T(1024)S(1)} fusion(f32[7680]{0:T(1024)S(1)} %reshape.222, s32[2048]{0:T(1024)S(1)} %get-tuple-element.19), kind=kCustom, calls=%fused_computation.11 | custom fusion | bytes 24576 | tf_op jit(solution)/shard_map/gather | solution.py:31
  368.6 11.3 %scatter_custom_fusion.7 = f32[7680]{0:T(1024)S(1)} fusion(s32[2048]{0:T(1024)S(1)} %get-tuple-element.20, f32[2048]{0:T(1024)S(1)} %add_multiply_fusion, f32[]{:T(128)} %constant.40.clone.1), kind=kCustom, calls=%fused_computation.72 | custom fusion | flops 2048 | bytes 30724 | tf_op jit(solution)/shard_map/scatter-add | solution.py:40
  380.1 0.9 reduce.24
  381.8 5.9 %all-to-all-start.8 = ((f32[8,1,960]{2,1,0:T(1,128)}), f32[8,1,960]{2,1,0:T(1,128)S(1)}, u32[]{:S(2)}, u32[]{:S(2)}) async-start(f32[8,1,960]{2,1,0:T(1,128)} %reshape.467), calls=%async_computation.8 | async-start | bytes 65536 | tf_op jit(solution)/shard_map/all_to_all | solution.py:43
  387.7 11.3 %scatter_custom_fusion.6 = f32[7680]{0:T(1024)S(1)} fusion(s32[2048]{0:T(1024)S(1)} %get-tuple-element.32, f32[2048]{0:T(1024)S(1)} %add_multiply_fusion, f32[]{:T(128)} %constant.40.clone.1), kind=kCustom, calls=%fused_computation.74 | custom fusion | flops 2048 | bytes 30724 | tf_op jit(solution)/shard_map/scatter-add | solution.py:37
  400.3 10.7 %all-reduce.1 = (f32[30,256]{1,0:T(8,128)S(1)}, f32[30,256]{1,0:T(8,128)S(1)}) all-reduce(f32[30,256]{1,0:T(8,128)S(1)} %reshape.223, f32[30,256]{1,0:T(8,128)S(1)} %reshape.226), channel_id=1, replica_groups=mesh['geo'=8,'rep'=4] {'rep'}, use_global_device_ids=true, to_apply=%region_28.30 | all-reduce | flops 15360 | bytes 122880 | tf_op jit(solution)/shard_map/psum | solution.py:45
  413.6 22.3 %psum.111 = f32[]{:T(128)} all-reduce(f32[]{:T(128)S(6)} %add.173), channel_id=1, replica_groups=mesh['geo'=8,'rep'=4] {'geo'}, use_global_device_ids=true, to_apply=%region_33.35 | all-reduce | flops 1 | bytes 8 | tf_op jit(solution)/shard_map/psum | solution.py:68
  (119 shorter events, 28.6 us)
Async XLA Ops:
  0.6 0.7 copy-start.7
  2.0 13.7 %all-to-all-start = ((s32[8,1,1]{2,1,0:T(1,128)}), s32[8,1,1]{2,1,0:T(1,128)S(1)}, u32[]{:S(2)}, u32[]{:S(2)}) async-start(s32[8,1,1]{2,1,0:T(1,128)} %copy.79), calls=%async_computation | async-start | bytes 8192 | tf_op jit(solution)/shard_map/all_to_all | solution.py:16
  18.9 3.5 copy-start.3
  18.9 3.5 copy-start.4
  19.0 3.5 copy-start.5
  19.0 16.1 %all-to-all-start.1 = ((f32[8,1,960]{2,1,0:T(1,128)}), f32[8,1,960]{2,1,0:T(1,128)S(1)}, u32[]{:S(2)}, u32[]{:S(2)}) async-start(f32[8,1,960]{2,1,0:T(1,128)} %reshape.453), calls=%async_computation.1 | async-start | bytes 65536 | tf_op jit(solution)/shard_map/all_to_all | solution.py:51
  22.5 0.8 copy-start
  36.3 11.8 %copy-start.6 = (f32[2048]{0:T(1024)S(1)}, f32[2048]{0:T(1024)}, u32[]{:S(2)}) copy-start(f32[2048]{0:T(1024)} %param.11) | copy-start | bytes 24580
  61.4 17.2 %all-to-all-start.2 = ((f32[8,1,960]{2,1,0:T(1,128)}), f32[8,1,960]{2,1,0:T(1,128)S(1)}, u32[]{:S(2)}, u32[]{:S(2)}) async-start(f32[8,1,960]{2,1,0:T(1,128)} %reshape.455), calls=%async_computation.2 | async-start | bytes 65536 | tf_op jit(solution)/shard_map/all_to_all | solution.py:43
  79.9 10.7 %copy-start.1 = (f32[30,256]{1,0:T(8,128)S(1)}, f32[30,256]{1,0:T(8,128)}, u32[]{:S(2)}) copy-start(f32[30,256]{1,0:T(8,128)} %param.19) | copy-start | bytes 92164
  79.9 10.7 %copy-start.2 = (f32[30,256]{1,0:T(8,128)S(1)}, f32[30,256]{1,0:T(8,128)}, u32[]{:S(2)}) copy-start(f32[30,256]{1,0:T(8,128)} %param.18) | copy-start | bytes 92164
  93.9 17.8 %all-to-all-start.3 = ((f32[8,1,960]{2,1,0:T(1,128)}), f32[8,1,960]{2,1,0:T(1,128)S(1)}, u32[]{:S(2)}, u32[]{:S(2)}) async-start(f32[8,1,960]{2,1,0:T(1,128)} %reshape.457), calls=%async_computation.3 | async-start | bytes 65536 | tf_op jit(solution)/shard_map/all_to_all | solution.py:62
  138.0 18.8 %all-to-all-start.4 = ((f32[8,1,960]{2,1,0:T(1,128)}), f32[8,1,960]{2,1,0:T(1,128)S(1)}, u32[]{:S(2)}, u32[]{:S(2)}) async-start(f32[8,1,960]{2,1,0:T(1,128)} %reshape.459), calls=%async_computation.4 | async-start | bytes 65536 | tf_op jit(solution)/shard_map/all_to_all | solution.py:43
  219.2 15.2 %all-to-all-start.5 = ((f32[8,1,960]{2,1,0:T(1,128)}), f32[8,1,960]{2,1,0:T(1,128)S(1)}, u32[]{:S(2)}, u32[]{:S(2)}) async-start(f32[8,1,960]{2,1,0:T(1,128)} %reshape.461), calls=%async_computation.5 | async-start | bytes 65536 | tf_op jit(solution)/shard_map/all_to_all | solution.py:62
  260.7 17.2 %all-to-all-start.6 = ((f32[8,1,960]{2,1,0:T(1,128)}), f32[8,1,960]{2,1,0:T(1,128)S(1)}, u32[]{:S(2)}, u32[]{:S(2)}) async-start(f32[8,1,960]{2,1,0:T(1,128)} %reshape.463), calls=%async_computation.6 | async-start | bytes 65536 | tf_op jit(solution)/shard_map/all_to_all | solution.py:43
  340.3 15.2 %all-to-all-start.7 = ((f32[8,1,960]{2,1,0:T(1,128)}), f32[8,1,960]{2,1,0:T(1,128)S(1)}, u32[]{:S(2)}, u32[]{:S(2)}) async-start(f32[8,1,960]{2,1,0:T(1,128)} %reshape.465), calls=%async_computation.7 | async-start | bytes 65536 | tf_op jit(solution)/shard_map/all_to_all | solution.py:62
  381.8 17.2 %all-to-all-start.8 = ((f32[8,1,960]{2,1,0:T(1,128)}), f32[8,1,960]{2,1,0:T(1,128)S(1)}, u32[]{:S(2)}, u32[]{:S(2)}) async-start(f32[8,1,960]{2,1,0:T(1,128)} %reshape.467), calls=%async_computation.8 | async-start | bytes 65536 | tf_op jit(solution)/shard_map/all_to_all | solution.py:43
where the time goes:
time: 440 us; the launch traced here: 439 us
  blocking collectives  145 us (33%)
  other arithmetic  112 us (25%)
  local copies, waits for them, and re-layouts  111 us (25%)
  starting transfers between devices  47.2 us (11%)
  between operations  16.1 us (4%)
  waiting for transfers between devices  5.55 us (1%)
    psum x3, blocking collectives, squares(): return lax.psum(local, 'geo')  57.7 us
    gather x4, local copies, waits for them, and re-layouts, pick(): return fetched.reshape(-1)[work_index]  47.1 us
    scatter-add x4, other arithmetic, totals(): jax.ops.segment_sum(values, res_index, num_segments=cells * tracts_dev)  45.2 us
    scatter-add x4, other arithmetic, totals(): jax.ops.segment_sum(values, work_index, num_segments=slot_count)  45.1 us
    psum x2, blocking collectives, body(): alpha = norm_now / lax.psum(local_curv, 'geo')  44.7 us
    psum x4, blocking collectives, totals(): return lax.psum((res_part, folded.reshape(cells, tracts_dev)), 'rep')  42.8 us
    gather x3, local copies, waits for them, and re-layouts, body(): along = dir_res.reshape(-1)[res_index] + pick(dir_piece)  35.3 us
    all_to_all x4, starting transfers between devices, totals(): lax.all_to_all(work_part, 'geo', split_axis=0, concat_axis=0, tiled=True)  23.8 us
  transfers between devices with their start and end apart: 9, of which 1 were waited for; matrix products, arithmetic and copies ran while one was open for 21% of the time, Pallas kernels for 0%

commit v1 on v0

v1 whole, which is shorter than its diff:
```python
import functools

import jax
import jax.numpy as jnp
from jax import lax
from jax.experimental import pallas as pl
from jax.experimental.pallas import tpu as pltpu
from jax.sharding import PartitionSpec as P

BLK = 32
ITERS = 3
RIDGE = 0.5
LANES = 128
TABLE_BYTES = 8 << 20
ALL = ("geo", "rep")

F32 = jnp.float32
BF16 = jnp.bfloat16


def start_plan(base, job_res, job_slot, job_cell, needed, lam_res, lam_work, target_res, target_work):
    cells, tracts_dev = lam_res.shape
    blocks_dev = tracts_dev // BLK
    requests = lax.all_to_all(needed[0], "geo", split_axis=0, concat_axis=0, tiled=True)
    sources, listed = requests.shape
    onehot = (
        requests[:, :, None] == jnp.arange(blocks_dev, dtype=jnp.int32)[None, None, :]
    ).astype(jnp.float32)
    slot_shape = (sources, listed, cells, BLK)
    slot_count = sources * listed * cells * BLK
    res_index = job_cell * tracts_dev + job_res
    work_index = (job_slot // BLK * cells + job_cell) * BLK + job_slot % BLK

    def serve(table):
        blocks = table.reshape(cells, blocks_dev, BLK).transpose(1, 0, 2)
        return jnp.take(blocks, requests, axis=0)

    def pick(fetched):
        return fetched.reshape(-1)[work_index]

    def fold(arrived):
        return jnp.einsum("skb,skcx->cbx", onehot, arrived, precision=lax.Precision.HIGHEST)

    def totals(values):
        res_part = jax.ops.segment_sum(values, res_index, num_segments=cells * tracts_dev).reshape(
            cells, tracts_dev
        )
        work_part = jax.ops.segment_sum(values, work_index, num_segments=slot_count).reshape(
            slot_shape
        )
        arrived = lax.all_to_all(work_part, "geo", split_axis=0, concat_axis=0, tiled=True)
        folded = fold(arrived)
        return lax.psum((res_part, folded.reshape(cells, tracts_dev)), "rep")

    def inner(a_res, a_work, b_res, b_work):
        return lax.psum(jnp.sum(a_res * b_res) + jnp.sum(a_work * b_work), "geo")

    fetched_lam = lax.all_to_all(serve(lam_work), "geo", split_axis=0, concat_axis=0, tiled=True)
    weight = base * jnp.exp(lam_res.reshape(-1)[res_index] + pick(fetched_lam))
    total_res, total_work = totals(weight)
    resid_res = -(total_res - target_res)
    resid_work = -(total_work - target_work)
    norm = inner(resid_res, resid_work, resid_res, resid_work)
    zeros = jnp.zeros_like(resid_res)

    def turn(_, state):
        step_res, step_work, resid_res, resid_work, dir_res, dir_work, norm_now = state
        dir_piece = lax.all_to_all(serve(dir_work), "geo", split_axis=0, concat_axis=0, tiled=True)
        along = dir_res.reshape(-1)[res_index] + pick(dir_piece)
        image_res, image_work = totals(weight * along)
        image_res = image_res + RIDGE * dir_res
        image_work = image_work + RIDGE * dir_work
        alpha = norm_now / inner(dir_res, dir_work, image_res, image_work)
        step_res = step_res + alpha * dir_res
        step_work = step_work + alpha * dir_work
        resid_res = resid_res - alpha * image_res
        resid_work = resid_work - alpha * image_work
        norm_next = inner(resid_res, resid_work, resid_res, resid_work)
        dir_res = resid_res + norm_next / norm_now * dir_res
        dir_work = resid_work + norm_next / norm_now * dir_work
        return step_res, step_work, resid_res, resid_work, dir_res, dir_work, norm_next

    state = (zeros, zeros, resid_res, resid_work, resid_res, resid_work, norm)
    return lax.fori_loop(0, ITERS, turn, state)[:4]


def split2(x):
    high = x.astype(BF16)
    low = (x - high.astype(F32)).astype(BF16)
    return high, low


def split3(x):
    high = x.astype(BF16)
    rest = x - high.astype(F32)
    mid = rest.astype(BF16)
    low = (rest - mid.astype(F32)).astype(BF16)
    return high, mid, low


def dot_nt(a, b):
    return lax.dot_general(a, b, (((1,), (1,)), ((), ())), preferred_element_type=F32)


def dot_nn(a, b):
    return jnp.dot(a, b, preferred_element_type=F32)


def pack_kernel(dims, needed_ref, base_ref, res_ref, slot_ref, cell_ref, a_ref, b_ref, c_ref, d_ref, out_ref):
    devices, rows, cap, listed, cells = dims["devices"], dims["rows"], dims["cap"], dims["listed"], dims["cells"]
    tracts = a_ref.shape[1]
    jobs = cell_ref.shape[1]
    chunk = 256
    cell = cell_ref[...]
    member = lax.broadcasted_iota(jnp.int32, (devices, jobs), 0) == cell
    member_b = member.astype(F32).astype(BF16)
    before = lax.broadcasted_iota(jnp.int32, (chunk, chunk), 0) < lax.broadcasted_iota(jnp.int32, (chunk, chunk), 1)
    before = before.astype(F32).astype(BF16)
    ranks = []
    count = jnp.zeros((devices, 1), F32)
    for at in range(0, jobs, chunk):
        part = member_b[:, at : at + chunk]
        seen = dot_nn(part, before) + count
        own = member[:, at : at + chunk]
        ranks.append(jnp.sum(jnp.where(own, seen, 0.0), axis=0, keepdims=True))
        count = count + jnp.sum(own.astype(F32), axis=1, keepdims=True)
    rank = jnp.concatenate(ranks, axis=1).astype(jnp.int32)
    largest = jnp.max(count, axis=0, keepdims=True)
    chosen = lax.broadcasted_iota(jnp.int32, (cap, jobs), 0) == rank
    high, low = split2(base_ref[...])
    values = (res_ref[...].astype(F32), slot_ref[...].astype(F32), high.astype(F32), low.astype(F32))
    sent = [dot_nt(member_b, jnp.where(chosen, value, 0.0).astype(BF16)) for value in values]
    sent = (sent[0], sent[1], sent[2] + sent[3])

    def put(row, value):
        out_ref[pl.ds(row, devices, stride=rows), :] = value

    row = 0
    for value in sent:
        for at in range(0, cap, LANES):
            put(row, value[:, at : at + LANES])
            row += 1
    owner = lax.broadcasted_iota(jnp.int32, (devices, listed * BLK), 1) // BLK
    wanted = jnp.zeros((devices, listed * BLK), F32)
    for p in range(listed):
        wanted = jnp.where(owner == p, needed_ref[p].astype(F32), wanted)
    for at in range(0, listed * BLK, LANES):
        put(row, wanted[:, at : at + LANES])
        row += 1
    put(row, jnp.broadcast_to(largest, (devices, LANES)))
    row += 1
    rep = lax.axis_index("rep")
    mine = a_ref[...]
    for k, ref in enumerate((b_ref, c_ref, d_ref)):
        mine = jnp.where(rep == k + 1, ref[...], mine)
    mine = jnp.concatenate([mine, jnp.zeros((devices - cells, tracts), F32)], axis=0)
    for at in range(0, tracts, LANES):
        put(row, mine[:, at : at + LANES])
        row += 1


def swap_blocks(x):
    side, width = x.shape
    shift = (
        lax.broadcasted_iota(jnp.int32, (side, width), 0)
        - lax.broadcasted_iota(jnp.int32, (side, width), 1) // BLK
        + side
    ) % side
    out = x
    for d in range(1, side):
        moved = pltpu.roll(pltpu.roll(x, width - BLK * d, 1), d, 0)
        out = jnp.where(shift == d, moved, out)
    return out


def total(x):
    return jnp.sum(jnp.sum(x, axis=0, keepdims=True), axis=1, keepdims=True)


def cell_kernel(dims, in_ref, out_ref, flag_ref, hi_ref, lo_ref):
    devices, rows, cap, groups, reps, tracts, slots, sent_rows = (
        dims[k] for k in ("devices", "rows", "cap", "groups", "reps", "tracts", "slots", "sent_rows")
    )
    per = cap // LANES

    def row_of(row, device):
        return in_ref[pl.ds(device * rows + row, 1), :]

    def group_rows(row, rep):
        return in_ref[pl.ds(rep * rows + row, groups, stride=rows * reps), :]

    def wide(row, rep, width):
        return jnp.concatenate([group_rows(row + k, rep) for k in range(width // LANES)], axis=1)

    at_res, at_slot, at_base, at_need = 0, per, 2 * per, 3 * per
    at_most = at_need + slots // LANES
    at_own = at_most + 1

    tract = lax.broadcasted_iota(jnp.int32, (tracts, LANES), 0).astype(F32)
    place = lax.broadcasted_iota(jnp.int32, (slots, LANES), 0).astype(F32)
    for g in range(groups):
        highs, lows, picks = [], [], []
        for r in range(reps):
            for k in range(per):
                device = g * reps + r
                high, low = split2(row_of(at_base + k, device))
                at_tract = tract == row_of(at_res + k, device)
                highs.append(jnp.where(at_tract, high.astype(F32), 0.0).astype(BF16))
                lows.append(jnp.where(at_tract, low.astype(F32), 0.0).astype(BF16))
                picks.append((place == row_of(at_slot + k, device)).astype(F32).astype(BF16))
        picked = jnp.concatenate(picks, axis=1)
        table = dot_nt(jnp.concatenate(highs, axis=1), picked) + dot_nt(jnp.concatenate(lows, axis=1), picked)
        high, low = split2(table)
        hi_ref[g] = high
        lo_ref[g] = low

    need = wide(at_need, 0, slots)
    lam_res = wide(at_own, 0, tracts)
    lam_work = swap_blocks(wide(at_own, 1, tracts))
    target_res = wide(at_own, 2, tracts)
    target_work = swap_blocks(wide(at_own, 3, tracts))

    block_row = lax.broadcasted_iota(jnp.int32, (groups, slots), 0).astype(F32)

    def fetch(v):
        out = jnp.zeros((groups, slots), F32)
        for b in range(groups):
            out = jnp.where(need == float(b), v[b : b + 1, :], out)
        return out

    def fold(u):
        out = jnp.zeros((groups, slots), F32)
        for g in range(groups):
            out = out + jnp.where(need[g : g + 1, :] == block_row, u[g : g + 1, :], 0.0)
        return out

    rise_res = jnp.exp(lam_res)
    rise_work = jnp.exp(fetch(lam_work))
    group_row = lax.broadcasted_iota(jnp.int32, (3 * groups, tracts), 0) % groups

    def spread(x):
        return jnp.concatenate([piece.astype(F32) for piece in split3(x)], axis=0)

    def across(u_res, u_list):
        left = spread(rise_work * u_list)
        right = spread(rise_res * u_res)
        to_res = jnp.zeros((3 * groups, tracts), F32)
        to_list = jnp.zeros((3 * groups, slots), F32)
        for g in range(groups):
            left_g = jnp.where(group_row == g, left, 0.0).astype(BF16)
            right_g = jnp.where(group_row == g, right, 0.0).astype(BF16)
            to_res = to_res + dot_nt(left_g, hi_ref[g]) + dot_nt(left_g, lo_ref[g])
            to_list = to_list + dot_nn(right_g, hi_ref[g]) + dot_nn(right_g, lo_ref[g])
        gather = lambda y: y[:groups] + y[groups : 2 * groups] + y[2 * groups :]
        return rise_res * gather(to_res), fold(rise_work * gather(to_list))

    ones = jnp.ones((groups, tracts), F32)
    total_res, total_work = across(ones, ones)
    diag = (total_res + RIDGE, total_work + RIDGE)
    resid = (target_res - total_res, target_work - total_work)

    def apply(v):
        far = across(v[0], fetch(v[1]))
        return tuple(d * x + y for d, x, y in zip(diag, v, far))

    def dot(a, b):
        return total(a[0] * b[0] + a[1] * b[1])

    def unit(w):
        square = dot(w, w)
        some = square > 0.0
        scale = jnp.where(some, lax.rsqrt(jnp.where(some, square, 1.0)), 0.0)
        return square * scale, tuple(x * scale for x in w)

    size, v = unit(resid)
    basis, entries = [v], [size]
    last, off = None, None
    for _ in range(ITERS):
        w = apply(v)
        along = dot(v, w)
        w = tuple(x - along * y for x, y in zip(w, v))
        if last is not None:
            w = tuple(x - off * y for x, y in zip(w, last))
        last = v
        off, v = unit(w)
        entries += [along, off]
        basis.append(v)

    def put(row, value):
        for r in range(reps):
            out_ref[pl.ds(r * sent_rows + row, groups, stride=reps * sent_rows), :] = value

    row = 0
    for v in basis:
        for part in (v[0], swap_blocks(v[1])):
            for at in range(0, tracts, LANES):
                put(row, part[:, at : at + LANES])
                row += 1
    lane = lax.broadcasted_iota(jnp.int32, (groups, LANES), 1)
    numbers = jnp.zeros((groups, LANES), F32)
    for k, entry in enumerate(entries):
        numbers = jnp.where(lane == k, entry, numbers)
    put(row, numbers)
    most = group_rows(at_most, 0)
    for r in range(1, reps):
        most = jnp.maximum(most, group_rows(at_most, r))
    flag_ref[...] = jnp.max(most, axis=0, keepdims=True)


def join_kernel(dims, in_ref, step_res_ref, step_work_ref, resid_res_ref, resid_work_ref):
    devices, sent_rows, tracts, cells = dims["devices"], dims["sent_rows"], dims["tracts"], dims["cells"]

    def take(row):
        return in_ref[pl.ds(row, devices, stride=sent_rows), :]

    numbers = take(sent_rows - 1)
    entry = lambda k: jnp.broadcast_to(numbers[:, k : k + 1], (devices, LANES))
    along = [entry(1 + 2 * k) for k in range(ITERS)]
    off = [entry(2 + 2 * k) for k in range(ITERS)]

    def inner(a, b):
        return jnp.sum(sum(x * y for x, y in zip(a, b)), axis=0, keepdims=True)

    resid = [entry(0)]
    direct = [entry(0)]
    step = []
    norm = inner(resid, resid)
    for turn in range(ITERS):
        image = []
        for k in range(turn + 2):
            value = None
            for term in ((off[k - 1], k - 1), (along[k] if k < ITERS else None, k), (off[k] if k < ITERS else None, k + 1)):
                if 0 <= term[1] <= turn:
                    product = term[0] * direct[term[1]]
                    value = product if value is None else value + product
            image.append(value)
        alpha = norm / inner(direct, image)
        step = [s + alpha * d for s, d in zip(step, direct)] + [alpha * d for d in direct[len(step) :]]
        resid = [r - alpha * i for r, i in zip(resid, image)] + [-alpha * i for i in image[len(resid) :]]
        following = inner(resid, resid)
        beta = following / norm
        direct = [r + beta * d for r, d in zip(resid, direct)] + resid[len(direct) :]
        norm = following

    half = tracts // LANES
    for part, (step_ref, resid_ref) in enumerate(((step_res_ref, resid_res_ref), (step_work_ref, resid_work_ref))):
        for at in range(half):
            vectors = [take((2 * k + part) * half + at) for k in range(ITERS + 1)]
            lanes = slice(at * LANES, (at + 1) * LANES)
            step_ref[:, lanes] = sum(s * v for s, v in zip(step, vectors))[:cells]
            resid_ref[:, lanes] = sum(r * v for r, v in zip(resid, vectors))[:cells]


def round_up(value, unit):
    return -(-value // unit) * unit


def plan_dims(mesh_shape, shapes):
    groups, reps = mesh_shape["geo"], mesh_shape["rep"]
    cells, tracts = shapes["lam"]
    listed = shapes["needed"][1] * shapes["needed"][2]
    slots = listed * BLK
    jobs = shapes["jobs"]
    cap = round_up(max(1, 3 * jobs // (2 * cells)), LANES)
    rows = round_up(3 * cap // LANES + slots // LANES + 1 + tracts // LANES, 8)
    fits = (
        groups * reps >= cells
        and reps == 4
        and groups == 8
        and listed == groups
        and slots == tracts
        and tracts % LANES == 0
        and tracts <= 256
        and jobs % 256 == 0
        and groups * tracts * slots * 4 <= TABLE_BYTES
    )
    return fits, dict(
        devices=groups * reps,
        groups=groups,
        reps=reps,
        cells=cells,
        tracts=tracts,
        slots=slots,
        listed=listed,
        cap=cap,
        rows=rows,
        sent_rows=2 * (ITERS + 1) * (tracts // LANES) + 1,
    )


def owner_plan(dims, base, job_res, job_slot, job_cell, needed, lam_res, lam_work, target_res, target_work):
    devices, rows, sent_rows, cells, tracts = (dims[k] for k in ("devices", "rows", "sent_rows", "cells", "tracts"))
    vmem = pl.BlockSpec(memory_space=pltpu.VMEM)
    smem = pl.BlockSpec(memory_space=pltpu.SMEM)
    flat = lambda x: x.reshape(1, -1)
    packed = pl.pallas_call(
        functools.partial(pack_kernel, dims),
        out_shape=jax.ShapeDtypeStruct((devices * rows, LANES), F32),
        in_specs=[smem] + [vmem] * 8,
        out_specs=vmem,
        name="pack",
    )(needed.reshape(-1), flat(base), flat(job_res), flat(job_slot), flat(job_cell), lam_res, lam_work, target_res, target_work)
    arrived = lax.all_to_all(packed.reshape(devices, rows, LANES), ALL, split_axis=0, concat_axis=0, tiled=True)
    sent, most = pl.pallas_call(
        functools.partial(cell_kernel, dims),
        out_shape=(
            jax.ShapeDtypeStruct((devices * sent_rows, LANES), F32),
            jax.ShapeDtypeStruct((1, LANES), F32),
        ),
        in_specs=[vmem],
        out_specs=(vmem, vmem),
        scratch_shapes=[pltpu.VMEM((dims["groups"], tracts, dims["slots"]), BF16)] * 2,
        name="cell",
    )(arrived.reshape(devices * rows, LANES))
    back = lax.all_to_all(sent.reshape(devices, sent_rows, 1, LANES), ALL, split_axis=0, concat_axis=0, tiled=True)
    outs = pl.pallas_call(
        functools.partial(join_kernel, dims),
        out_shape=(jax.ShapeDtypeStruct((cells, tracts), F32),) * 4,
        in_specs=[vmem],
        out_specs=(vmem,) * 4,
        name="join",
    )(back.reshape(devices * sent_rows, LANES))
    return outs, most[0, 0] > dims["cap"]


def body(mesh_shape, *args):
    base, needed, lam_res = args[0], args[4], args[5]
    fits, dims = plan_dims(mesh_shape, {"lam": lam_res.shape, "needed": needed.shape, "jobs": base.shape[0]})
    if not fits:
        return start_plan(*args)
    outs, over = owner_plan(dims, *args)
    return lax.cond(over, lambda: tuple(start_plan(*args)), lambda: tuple(outs))


def solution(mesh):
    in_specs = (P(ALL),) * 4 + (P("geo", None, None),) + (P(None, "geo"),) * 4
    out_specs = (P(None, "geo"),) * 4
    return jax.shard_map(
        functools.partial(body, dict(mesh.shape)), mesh=mesh, in_specs=in_specs, out_specs=out_specs, check_vma=False
    )
```

time: 440 us -> 47.2 us (0.11)
  blocking collectives: 145 us -> 15.6 us
  other arithmetic: 112 us -> 0 us
  local copies, waits for them, and re-layouts: 111 us -> 2.07 us
  starting transfers between devices: 47.2 us -> 2.59 us
  between operations: 16.1 us -> 0.96 us
  Pallas kernels: 0 us -> 14.9 us
  waiting for transfers between devices: 5.55 us -> 10.4 us
    psum x9 -> x0, blocking collectives: 145 us -> none  [the longest x3 57.7 us: squares(): return lax.psum(local, 'geo')]
    gather x12 -> x0, local copies, waits for them, and re-layouts: 96.5 us -> none  [the longest x4 47.1 us: pick(): return fetched.reshape(-1)[work_index]]
    scatter-add x8 -> x0, other arithmetic: 90.3 us -> none  [the longest x4 45.2 us: totals(): jax.ops.segment_sum(values, res_index, num_segments=cells * tracts_dev)]
    all_to_all x9 -> x1, starting transfers between devices: 47.2 us -> 2.59 us  [owner_plan(): lax.all_to_all(sent.reshape(devices, sent_rows, 1, LANES), ALL, split_axi...]
    all_to_all x0 -> x1, blocking collectives: none -> 15.6 us  [owner_plan(): lax.all_to_all(packed.reshape(devices, rows, LANES), ALL, split_axis=0, c...]
    pallas_call x0 -> x3, Pallas kernels: none -> 14.9 us  [the longest x1 10.4 us: owner_plan(): pl.pallas_call(functools.partial(cell_kernel, dims), out_shape=(jax.Shape...]
    unnamed x8 -> x0, other arithmetic: 7.58 us -> none
    unnamed x33 -> x22, local copies, waits for them, and re-layouts: 9.09 us -> 2.07 us
  transfers between devices with their start and end apart: 9 -> 1, of which waited for: 1 -> 1; matrix products, arithmetic and copies ran while one was open for 21% -> 0% of each run, Pallas kernels for 0% -> 0%
where the time goes in v1:
time: 47.2 us; the launch traced here: 46.8 us
  blocking collectives  15.6 us (33%)
  Pallas kernels  14.9 us (32%)
  waiting for transfers between devices  10.4 us (22%)
  starting transfers between devices  2.59 us (5%)
  local copies, waits for them, and re-layouts  2.07 us (4%)
  between operations  0.96 us (2%)
    all_to_all x1, blocking collectives, owner_plan(): lax.all_to_all(packed.reshape(devices, rows, LANES), ALL, split_axis=0, c...  15.6 us
    pallas_call x1, Pallas kernels, owner_plan(): pl.pallas_call(functools.partial(cell_kernel, dims), out_shape=(jax.Shape...  10.4 us
    all_to_all x1, waiting for transfers between devices, owner_plan(): lax.all_to_all(sent.reshape(devices, sent_rows, 1, LANES), ALL, split_axi...  10.4 us
    pallas_call x1, Pallas kernels, owner_plan(): pl.pallas_call(functools.partial(pack_kernel, dims), out_shape=jax.ShapeD...  2.66 us
    all_to_all x1, starting transfers between devices, owner_plan(): lax.all_to_all(sent.reshape(devices, sent_rows, 1, LANES), ALL, split_axi...  2.59 us
    unnamed x22, local copies, waits for them, and re-layouts  2.07 us
    pallas_call x1, Pallas kernels, owner_plan(): pl.pallas_call(functools.partial(join_kernel, dims), out_shape=(jax.Shape...  1.87 us
  transfers between devices with their start and end apart: 1, of which 1 were waited for; matrix products, arithmetic and copies ran while one was open for 0% of the time, Pallas kernels for 0%

profile of v1, /device:TPU:0, one launch (start us, length us, event | category | flops | bytes accessed | tf_op | source)
XLA Modules:
  0.0 46.8 jit_solution(4229211898504953296)
XLA Ops:
  0.6 0.0 copy-start.5
  0.6 0.0 copy-start.9
  0.7 0.7 %copy-done.5 = s32[2048]{0:T(1024)S(1)} copy-done((s32[2048]{0:T(1024)S(1)}, s32[2048]{0:T(1024)}, u32[]{:S(2)}) %copy-start.5) | copy-done | bytes 8216
  1.3 0.0 copy-done.9
  1.3 2.7 %pack.1 = f32[256,128]{1,0:T(8,128)} custom-call(s32[8]{0:T(128)S(1)} %bitcast.128, f32[1,2048]{1,0:T(1,128)} %bitcast.123, s32[1,2048]{1,0:T(1,128)S(1)} %bitcast.120, s32[1,2048]{1,0:T(1,128)} %bitcast.121, s32[1,2048]{1,0:T(1,128)} %bitcast.122, f32[30,256]{1,0:T(8,128)} %a_ref.1, f32[30,256]{1,0:T(8,128)} %b_ref.1, f32[30,256]{1,0:T(8,128)} %c_ref.1, ...), custom_call_target="tpu_custom_call" | custom-call | tf_op jit(solution)/shard_map/pack/pallas_call | solution.py:396
  4.0 15.6 %all_to_all.43 = f32[32,8,128]{2,1,0:T(8,128)} all-to-all(f32[32,8,128]{2,1,0:T(8,128)} %bitcast.113), channel_id=1, replica_groups=mesh['geo'=8,'rep'=4] {'geo','rep'}, dimensions={0} | all-to-all | bytes 262144 | tf_op jit(solution)/shard_map/all_to_all | solution.py:403
  19.6 10.4 %cell.1 = (f32[544,128]{1,0:T(8,128)}, f32[1,128]{1,0:T(1,128)}) custom-call(f32[256,128]{1,0:T(8,128)} %bitcast.112), custom_call_target="tpu_custom_call" | custom-call | tf_op jit(solution)/shard_map/cell/pallas_call | solution.py:404
  30.0 2.6 %all-to-all-start.6 = ((f32[32,17,1,128]{3,2,1,0:T(1,128)}), f32[32,17,1,128]{3,2,1,0:T(1,128)S(1)}, u32[]{:S(2)}, u32[]{:S(2)}) async-start(f32[32,17,1,128]{3,2,1,0:T(1,128)} %bitcast.119), calls=%async_computation.6 | async-start | bytes 557056 | tf_op jit(solution)/shard_map/all_to_all | solution.py:415
  32.6 0.0 copy-start.10
  32.6 0.6 %copy-done.10 = f32[1,128]{1,0:T(1,128)S(1)} copy-done((f32[1,128]{1,0:T(1,128)S(1)}, f32[1,128]{1,0:T(1,128)}, u32[]{:S(2)}) %copy-start.10) | copy-done | bytes 536
  33.3 10.4 %all-to-all-done.6 = f32[32,17,1,128]{3,2,1,0:T(1,128)S(1)} async-done(((f32[32,17,1,128]{3,2,1,0:T(1,128)}), f32[32,17,1,128]{3,2,1,0:T(1,128)S(1)}, u32[]{:S(2)}, u32[]{:S(2)}) %all-to-all-start.6) | async-done | bytes 278560 | tf_op jit(solution)/shard_map/all_to_all | solution.py:415
  43.7 0.0 copy-start
  43.7 0.7 %copy-done = f32[32,17,1,128]{3,2,1,0:T(1,128)} copy-done((f32[32,17,1,128]{3,2,1,0:T(1,128)}, f32[32,17,1,128]{3,2,1,0:T(1,128)S(1)}, u32[]{:S(2)}) %copy-start) | copy-done | bytes 278552
  44.4 0.0 copy-start.1
  44.4 0.0 copy-start.2
  44.4 0.0 copy-start.3
  44.4 0.0 copy-start.4
  44.4 0.0 copy-start.6
  44.4 0.0 copy-start.7
  44.4 0.0 copy-start.8
  44.4 1.9 %join.1 = (f32[30,256]{1,0:T(8,128)}, f32[30,256]{1,0:T(8,128)}, f32[30,256]{1,0:T(8,128)}, f32[30,256]{1,0:T(8,128)}) custom-call(f32[544,128]{1,0:T(8,128)} %bitcast.108), custom_call_target="tpu_custom_call" | custom-call | tf_op jit(solution)/shard_map/join/pallas_call | solution.py:416
  46.3 0.0 copy-done.1
  46.3 0.0 copy-done.2
  46.3 0.0 copy-done.3
  46.3 0.0 copy-done.4
  46.3 0.0 copy-done.6
  46.3 0.0 copy-done.7
  46.4 0.0 copy-done.8
  46.4 0.2 conditional.1
Async XLA Ops:
  0.6 0.7 %copy-start.5 = (s32[2048]{0:T(1024)S(1)}, s32[2048]{0:T(1024)}, u32[]{:S(2)}) copy-start(s32[2048]{0:T(1024)} %param.16) | copy-start | bytes 24580
  0.6 0.7 %copy-start.9 = (s32[1,8,1]{1,2,0:T(1,128)S(1)}, s32[1,8,1]{1,2,0:T(1,128)}, u32[]{:S(2)}) copy-start(s32[1,8,1]{1,2,0:T(1,128)} %param.19) | copy-start | bytes 100
  30.0 13.7 %all-to-all-start.6 = ((f32[32,17,1,128]{3,2,1,0:T(1,128)}), f32[32,17,1,128]{3,2,1,0:T(1,128)S(1)}, u32[]{:S(2)}, u32[]{:S(2)}) async-start(f32[32,17,1,128]{3,2,1,0:T(1,128)} %bitcast.119), calls=%async_computation.6 | async-start | bytes 557056 | tf_op jit(solution)/shard_map/all_to_all | solution.py:415
  32.6 0.7 %copy-start.10 = (f32[1,128]{1,0:T(1,128)S(1)}, f32[1,128]{1,0:T(1,128)}, u32[]{:S(2)}) copy-start(f32[1,128]{1,0:T(1,128)} %get-tuple-element.112) | copy-start | bytes 1540
  43.7 0.7 %copy-start = (f32[32,17,1,128]{3,2,1,0:T(1,128)}, f32[32,17,1,128]{3,2,1,0:T(1,128)S(1)}, u32[]{:S(2)}) copy-start(f32[32,17,1,128]{3,2,1,0:T(1,128)S(1)} %all-to-all-done.6) | copy-start | bytes 835588
  44.4 1.9 %copy-start.1 = (f32[30,256]{1,0:T(8,128)S(1)}, f32[30,256]{1,0:T(8,128)}, u32[]{:S(2)}) copy-start(f32[30,256]{1,0:T(8,128)} %b_ref.1) | copy-start | bytes 92164
  44.4 1.9 %copy-start.2 = (f32[30,256]{1,0:T(8,128)S(1)}, f32[30,256]{1,0:T(8,128)}, u32[]{:S(2)}) copy-start(f32[30,256]{1,0:T(8,128)} %a_ref.1) | copy-start | bytes 92164
  44.4 1.9 %copy-start.3 = (f32[30,256]{1,0:T(8,128)S(1)}, f32[30,256]{1,0:T(8,128)}, u32[]{:S(2)}) copy-start(f32[30,256]{1,0:T(8,128)} %c_ref.1) | copy-start | bytes 92164
  44.4 1.9 %copy-start.4 = (f32[30,256]{1,0:T(8,128)S(1)}, f32[30,256]{1,0:T(8,128)}, u32[]{:S(2)}) copy-start(f32[30,256]{1,0:T(8,128)} %d_ref.1) | copy-start | bytes 92164
  44.4 1.9 %copy-start.6 = (s32[2048]{0:T(1024)S(1)}, s32[2048]{0:T(1024)}, u32[]{:S(2)}) copy-start(s32[2048]{0:T(1024)} %param.17) | copy-start | bytes 24580
  44.4 1.9 %copy-start.7 = (s32[2048]{0:T(1024)S(1)}, s32[2048]{0:T(1024)}, u32[]{:S(2)}) copy-start(s32[2048]{0:T(1024)} %param.18) | copy-start | bytes 24580
  44.4 1.9 %copy-start.8 = (f32[2048]{0:T(1024)S(1)}, f32[2048]{0:T(1024)}, u32[]{:S(2)}) copy-start(f32[2048]{0:T(1024)} %param.15) | copy-start | bytes 24580

commit v2 on v1

--- a/solution.py
+++ b/solution.py
@@ -11,7 +11,6 @@
 ITERS = 3
 RIDGE = 0.5
 LANES = 128
-TABLE_BYTES = 8 << 20
 ALL = ("geo", "rep")
 
 F32 = jnp.float32
@@ -82,12 +81,6 @@
 
     state = (zeros, zeros, resid_res, resid_work, resid_res, resid_work, norm)
     return lax.fori_loop(0, ITERS, turn, state)[:4]
-
-
-def split2(x):
-    high = x.astype(BF16)
-    low = (x - high.astype(F32)).astype(BF16)
-    return high, low
 
 
 def split3(x):
@@ -126,20 +119,28 @@
         count = count + jnp.sum(own.astype(F32), axis=1, keepdims=True)
     rank = jnp.concatenate(ranks, axis=1).astype(jnp.int32)
     largest = jnp.max(count, axis=0, keepdims=True)
-    chosen = lax.broadcasted_iota(jnp.int32, (cap, jobs), 0) == rank
-    high, low = split2(base_ref[...])
-    values = (res_ref[...].astype(F32), slot_ref[...].astype(F32), high.astype(F32), low.astype(F32))
-    sent = [dot_nt(member_b, jnp.where(chosen, value, 0.0).astype(BF16)) for value in values]
-    sent = (sent[0], sent[1], sent[2] + sent[3])
+    chosen = (lax.broadcasted_iota(jnp.int32, (cap, jobs), 0) == rank).astype(F32).astype(BF16)
+    values = (res_ref[...].astype(F32), slot_ref[...].astype(F32)) + tuple(x.astype(F32) for x in split3(base_ref[...]))
+    held = jnp.concatenate([jnp.where(member, value, 0.0).astype(BF16) for value in values], axis=0)
+    moved = dot_nt(held, chosen)
+    moved = [moved[k * devices : (k + 1) * devices] for k in range(len(values))]
+    sent = (moved[0], moved[1], moved[2] + moved[3] + moved[4])
 
     def put(row, value):
         out_ref[pl.ds(row, devices, stride=rows), :] = value
 
     row = 0
     for value in sent:
-        for at in range(0, cap, LANES):
-            put(row, value[:, at : at + LANES])
-            row += 1
+        put(row, value)
+        row += 1
+    rep = lax.axis_index("rep")
+    mine = a_ref[...]
+    for k, ref in enumerate((b_ref, c_ref, d_ref)):
+        mine = jnp.where(rep == k + 1, ref[...], mine)
+    mine = jnp.concatenate([mine, jnp.zeros((devices - cells, tracts), F32)], axis=0)
+    for at in range(0, tracts, LANES):
+        put(row, mine[:, at : at + LANES])
+        row += 1
     owner = lax.broadcasted_iota(jnp.int32, (devices, listed * BLK), 1) // BLK
     wanted = jnp.zeros((devices, listed * BLK), F32)
     for p in range(listed):
@@ -148,173 +149,156 @@
         put(row, wanted[:, at : at + LANES])
         row += 1
     put(row, jnp.broadcast_to(largest, (devices, LANES)))
-    row += 1
-    rep = lax.axis_index("rep")
-    mine = a_ref[...]
-    for k, ref in enumerate((b_ref, c_ref, d_ref)):
-        mine = jnp.where(rep == k + 1, ref[...], mine)
-    mine = jnp.concatenate([mine, jnp.zeros((devices - cells, tracts), F32)], axis=0)
-    for at in range(0, tracts, LANES):
-        put(row, mine[:, at : at + LANES])
-        row += 1
-
-
-def swap_blocks(x):
-    side, width = x.shape
-    shift = (
-        lax.broadcasted_iota(jnp.int32, (side, width), 0)
-        - lax.broadcasted_iota(jnp.int32, (side, width), 1) // BLK
-        + side
-    ) % side
-    out = x
-    for d in range(1, side):
-        moved = pltpu.roll(pltpu.roll(x, width - BLK * d, 1), d, 0)
-        out = jnp.where(shift == d, moved, out)
-    return out
-
-
-def total(x):
-    return jnp.sum(jnp.sum(x, axis=0, keepdims=True), axis=1, keepdims=True)
-
-
-def cell_kernel(dims, in_ref, out_ref, flag_ref, hi_ref, lo_ref):
-    devices, rows, cap, groups, reps, tracts, slots, sent_rows = (
-        dims[k] for k in ("devices", "rows", "cap", "groups", "reps", "tracts", "slots", "sent_rows")
-    )
-    per = cap // LANES
+
+
+def cell_kernel(dims, in_ref, out_ref, flag_ref, pick_ref, mask_ref, weight_ref, hot_ref, turn_ref):
+    rows, groups, reps, sent_rows = (dims[k] for k in ("rows", "groups", "reps", "sent_rows"))
+    at_res, at_slot, at_base, at_own, at_need, at_most = 0, 1, 2, 3, 5, 7
+    tile = (groups, LANES)
+    sub = lax.broadcasted_iota(jnp.int32, tile, 0)
+    segment = lax.broadcasted_iota(jnp.int32, tile, 1) // BLK
+
+    side = LANES // BLK
 
     def row_of(row, device):
-        return in_ref[pl.ds(device * rows + row, 1), :]
-
-    def group_rows(row, rep):
-        return in_ref[pl.ds(rep * rows + row, groups, stride=rows * reps), :]
-
-    def wide(row, rep, width):
-        return jnp.concatenate([group_rows(row + k, rep) for k in range(width // LANES)], axis=1)
-
-    at_res, at_slot, at_base, at_need = 0, per, 2 * per, 3 * per
-    at_most = at_need + slots // LANES
-    at_own = at_most + 1
-
-    tract = lax.broadcasted_iota(jnp.int32, (tracts, LANES), 0).astype(F32)
-    place = lax.broadcasted_iota(jnp.int32, (slots, LANES), 0).astype(F32)
+        return jnp.broadcast_to(in_ref[pl.ds(device * rows + row, 1), :], tile)
+
+    def shifted(x, segments):
+        return pltpu.roll(x, BLK * (segments % side), 1) if segments % side else x
+
+    def unfold(row, rep, place):
+        tiles = []
+        for half in range(groups // side):
+            x = in_ref[pl.ds(rep * rows + row + half, groups, stride=reps * rows), :]
+            tiles += [shifted(x, place - k) for k in range(side)]
+        return tiles
+
+    def turned(tiles, slot):
+        for b, x in enumerate(tiles):
+            turn_ref[slot, pl.ds(b, groups, stride=groups), :] = x
+        return [turn_ref[slot, pl.ds(g * groups, groups), :] for g in range(groups)]
+
+    def both(res_rep, work_rep, slot):
+        res, work = turned(unfold(at_own, res_rep, 0), slot), unfold(at_own, work_rep, 1)
+        return [jnp.where(segment == 0, x, jnp.where(segment == 1, y, 0.0)) for x, y in zip(res, work)]
+
+    need = [jnp.where(segment == 1, x, -1.0) for x in turned(unfold(at_need, 0, 1), 0)]
+
+    def fetch(v):
+        tables = []
+        for g in range(groups):
+            table = jnp.where(segment == 0, v[g], 0.0)
+            for b in range(groups):
+                table = jnp.where(need[g] == float(b), v[b], table)
+            tables.append(table)
+        return tables
+
+    low = lax.broadcasted_iota(jnp.int32, (BLK, LANES), 0)
     for g in range(groups):
-        highs, lows, picks = [], [], []
         for r in range(reps):
-            for k in range(per):
+            device = g * reps + r
+            res = row_of(at_res, device).astype(jnp.int32)
+            slot = row_of(at_slot, device).astype(jnp.int32)
+            pick_ref[device, :groups, :] = res % BLK
+            pick_ref[device, groups:, :] = slot % BLK + BLK
+            mask_ref[device, :groups, :] = (res // BLK == sub).astype(F32)
+            mask_ref[device, groups:, :] = (slot // BLK == sub).astype(F32)
+            lanes = slice(r * LANES, (r + 1) * LANES)
+            hot_ref[g, :BLK, lanes] = (low == (res % BLK)[:1]).astype(F32).astype(BF16)
+            hot_ref[g, BLK:, lanes] = (low == (slot % BLK)[:1]).astype(F32).astype(BF16)
+
+    def along(device, table):
+        picked = jnp.take_along_axis(table, pick_ref[device, :groups, :], axis=1) * mask_ref[device, :groups, :]
+        picked += jnp.take_along_axis(table, pick_ref[device, groups:, :], axis=1) * mask_ref[device, groups:, :]
+        return jnp.broadcast_to(jnp.sum(picked, axis=0, keepdims=True), tile)
+
+    empty = jnp.zeros((2 * groups, LANES - 2 * BLK), F32)
+
+    def scatter(values):
+        res, folded = [], [jnp.zeros(tile, F32)] * groups
+        for g in range(groups):
+            columns = []
+            for r in range(reps):
                 device = g * reps + r
-                high, low = split2(row_of(at_base + k, device))
-                at_tract = tract == row_of(at_res + k, device)
-                highs.append(jnp.where(at_tract, high.astype(F32), 0.0).astype(BF16))
-                lows.append(jnp.where(at_tract, low.astype(F32), 0.0).astype(BF16))
-                picks.append((place == row_of(at_slot + k, device)).astype(F32).astype(BF16))
-        picked = jnp.concatenate(picks, axis=1)
-        table = dot_nt(jnp.concatenate(highs, axis=1), picked) + dot_nt(jnp.concatenate(lows, axis=1), picked)
-        high, low = split2(table)
-        hi_ref[g] = high
-        lo_ref[g] = low
-
-    need = wide(at_need, 0, slots)
-    lam_res = wide(at_own, 0, tracts)
-    lam_work = swap_blocks(wide(at_own, 1, tracts))
-    target_res = wide(at_own, 2, tracts)
-    target_work = swap_blocks(wide(at_own, 3, tracts))
-
-    block_row = lax.broadcasted_iota(jnp.int32, (groups, slots), 0).astype(F32)
-
-    def fetch(v):
-        out = jnp.zeros((groups, slots), F32)
-        for b in range(groups):
-            out = jnp.where(need == float(b), v[b : b + 1, :], out)
-        return out
-
-    def fold(u):
-        out = jnp.zeros((groups, slots), F32)
-        for g in range(groups):
-            out = out + jnp.where(need[g : g + 1, :] == block_row, u[g : g + 1, :], 0.0)
-        return out
-
-    rise_res = jnp.exp(lam_res)
-    rise_work = jnp.exp(fetch(lam_work))
-    group_row = lax.broadcasted_iota(jnp.int32, (3 * groups, tracts), 0) % groups
-
-    def spread(x):
-        return jnp.concatenate([piece.astype(F32) for piece in split3(x)], axis=0)
-
-    def across(u_res, u_list):
-        left = spread(rise_work * u_list)
-        right = spread(rise_res * u_res)
-        to_res = jnp.zeros((3 * groups, tracts), F32)
-        to_list = jnp.zeros((3 * groups, slots), F32)
-        for g in range(groups):
-            left_g = jnp.where(group_row == g, left, 0.0).astype(BF16)
-            right_g = jnp.where(group_row == g, right, 0.0).astype(BF16)
-            to_res = to_res + dot_nt(left_g, hi_ref[g]) + dot_nt(left_g, lo_ref[g])
-            to_list = to_list + dot_nn(right_g, hi_ref[g]) + dot_nn(right_g, lo_ref[g])
-        gather = lambda y: y[:groups] + y[groups : 2 * groups] + y[2 * groups :]
-        return rise_res * gather(to_res), fold(rise_work * gather(to_list))
-
-    ones = jnp.ones((groups, tracts), F32)
-    total_res, total_work = across(ones, ones)
-    diag = (total_res + RIDGE, total_work + RIDGE)
-    resid = (target_res - total_res, target_work - total_work)
+                mask = mask_ref[device]
+                parts = [jnp.concatenate([x.astype(F32)] * 2, axis=0) * mask for x in split3(values[device])]
+                columns.append(jnp.concatenate(parts, axis=0).astype(BF16))
+            sums = dot_nt(jnp.concatenate(columns, axis=1), hot_ref[g])
+            sums = sums[: 2 * groups] + sums[2 * groups : 4 * groups] + sums[4 * groups :]
+            sums = jnp.concatenate([sums, empty], axis=1)
+            res.append(jnp.where(segment == 0, sums[:groups], 0.0))
+            for b in range(groups):
+                folded[b] = folded[b] + jnp.where(need[g] == float(b), sums[groups:], 0.0)
+        return [x + y for x, y in zip(res, folded)]
+
+    lam = fetch(both(0, 1, 1))
+    weights = []
+    for device in range(groups * reps):
+        weight = row_of(at_base, device) * jnp.exp(along(device, lam[device // reps]))
+        weight_ref[device] = weight
+        weights.append(weight)
+    resid = [x - y for x, y in zip(both(2, 3, 2), scatter(weights))]
 
     def apply(v):
-        far = across(v[0], fetch(v[1]))
-        return tuple(d * x + y for d, x, y in zip(diag, v, far))
+        tables = fetch(v)
+        image = scatter([weight_ref[device] * along(device, tables[device // reps]) for device in range(groups * reps)])
+        return [x + RIDGE * y for x, y in zip(image, v)]
 
     def dot(a, b):
-        return total(a[0] * b[0] + a[1] * b[1])
+        products = [x * y for x, y in zip(a, b)]
+        while len(products) > 1:
+            products = [x + y for x, y in zip(products[::2], products[1::2])]
+        return jnp.sum(jnp.sum(products[0], axis=0, keepdims=True), axis=1, keepdims=True)
 
     def unit(w):
         square = dot(w, w)
         some = square > 0.0
         scale = jnp.where(some, lax.rsqrt(jnp.where(some, square, 1.0)), 0.0)
-        return square * scale, tuple(x * scale for x in w)
+        return square * scale, [x * scale for x in w]
 
     size, v = unit(resid)
     basis, entries = [v], [size]
     last, off = None, None
     for _ in range(ITERS):
         w = apply(v)
-        along = dot(v, w)
-        w = tuple(x - along * y for x, y in zip(w, v))
         if last is not None:
-            w = tuple(x - off * y for x, y in zip(w, last))
+            w = [x - off * y for x, y in zip(w, last)]
+        middle = dot(v, w)
+        w = [x - middle * y for x, y in zip(w, v)]
         last = v
         off, v = unit(w)
-        entries += [along, off]
+        entries += [middle, off]
         basis.append(v)
 
     def put(row, value):
         for r in range(reps):
             out_ref[pl.ds(r * sent_rows + row, groups, stride=reps * sent_rows), :] = value
 
-    row = 0
-    for v in basis:
-        for part in (v[0], swap_blocks(v[1])):
-            for at in range(0, tracts, LANES):
-                put(row, part[:, at : at + LANES])
-                row += 1
-    lane = lax.broadcasted_iota(jnp.int32, (groups, LANES), 1)
-    numbers = jnp.zeros((groups, LANES), F32)
+    for k, v in enumerate(basis):
+        for part, tiles in enumerate((turned(v, 3 + k), v)):
+            for half in range(groups // side):
+                row = jnp.zeros(tile, F32)
+                for q in range(side):
+                    row = jnp.where(segment == q, shifted(tiles[half * side + q], q - part), row)
+                put((2 * k + part) * (groups // side) + half, row)
+    lane = lax.broadcasted_iota(jnp.int32, tile, 1)
+    numbers = jnp.zeros(tile, F32)
     for k, entry in enumerate(entries):
         numbers = jnp.where(lane == k, entry, numbers)
-    put(row, numbers)
-    most = group_rows(at_most, 0)
-    for r in range(1, reps):
-        most = jnp.maximum(most, group_rows(at_most, r))
+    put(sent_rows - 1, numbers)
+    most = in_ref[pl.ds(at_most, groups * reps, stride=rows), :]
     flag_ref[...] = jnp.max(most, axis=0, keepdims=True)
 
 
 def join_kernel(dims, in_ref, step_res_ref, step_work_ref, resid_res_ref, resid_work_ref):
-    devices, sent_rows, tracts, cells = dims["devices"], dims["sent_rows"], dims["tracts"], dims["cells"]
+    devices, sent_rows, groups, cells = dims["devices"], dims["sent_rows"], dims["groups"], dims["cells"]
+    tile = (devices, LANES)
 
     def take(row):
         return in_ref[pl.ds(row, devices, stride=sent_rows), :]
 
     numbers = take(sent_rows - 1)
-    entry = lambda k: jnp.broadcast_to(numbers[:, k : k + 1], (devices, LANES))
+    entry = lambda k: jnp.broadcast_to(numbers[:, k : k + 1], tile)
     along = [entry(1 + 2 * k) for k in range(ITERS)]
     off = [entry(2 + 2 * k) for k in range(ITERS)]
 
@@ -342,7 +326,7 @@
         direct = [r + beta * d for r, d in zip(resid, direct)] + resid[len(direct) :]
         norm = following
 
-    half = tracts // LANES
+    half = groups * BLK // LANES
     for part, (step_ref, resid_ref) in enumerate(((step_res_ref, resid_res_ref), (step_work_ref, resid_work_ref))):
         for at in range(half):
             vectors = [take((2 * k + part) * half + at) for k in range(ITERS + 1)]
@@ -362,17 +346,15 @@
     slots = listed * BLK
     jobs = shapes["jobs"]
     cap = round_up(max(1, 3 * jobs // (2 * cells)), LANES)
-    rows = round_up(3 * cap // LANES + slots // LANES + 1 + tracts // LANES, 8)
+    rows = 8
     fits = (
         groups * reps >= cells
         and reps == 4
         and groups == 8
         and listed == groups
-        and slots == tracts
-        and tracts % LANES == 0
-        and tracts <= 256
+        and tracts == groups * BLK
+        and cap == LANES
         and jobs % 256 == 0
-        and groups * tracts * slots * 4 <= TABLE_BYTES
     )
     return fits, dict(
         devices=groups * reps,
@@ -380,16 +362,17 @@
         reps=reps,
         cells=cells,
         tracts=tracts,
-        slots=slots,
         listed=listed,
         cap=cap,
         rows=rows,
-        sent_rows=2 * (ITERS + 1) * (tracts // LANES) + 1,
+        sent_rows=2 * groups + 1,
     )
 
 
 def owner_plan(dims, base, job_res, job_slot, job_cell, needed, lam_res, lam_work, target_res, target_work):
-    devices, rows, sent_rows, cells, tracts = (dims[k] for k in ("devices", "rows", "sent_rows", "cells", "tracts"))
+    devices, rows, sent_rows, cells, tracts, groups, reps = (
+        dims[k] for k in ("devices", "rows", "sent_rows", "cells", "tracts", "groups", "reps")
+    )
     vmem = pl.BlockSpec(memory_space=pltpu.VMEM)
     smem = pl.BlockSpec(memory_space=pltpu.SMEM)
     flat = lambda x: x.reshape(1, -1)
@@ -409,7 +392,13 @@
         ),
         in_specs=[vmem],
         out_specs=(vmem, vmem),
-        scratch_shapes=[pltpu.VMEM((dims["groups"], tracts, dims["slots"]), BF16)] * 2,
+        scratch_shapes=[
+            pltpu.VMEM((devices, 2 * groups, LANES), jnp.int32),
+            pltpu.VMEM((devices, 2 * groups, LANES), F32),
+            pltpu.VMEM((devices, groups, LANES), F32),
+            pltpu.VMEM((groups, 2 * BLK, reps * LANES), BF16),
+            pltpu.VMEM((3 + ITERS + 1, groups * groups, LANES), F32),
+        ],
         name="cell",
     )(arrived.reshape(devices * rows, LANES))
     back = lax.all_to_all(sent.reshape(devices, sent_rows, 1, LANES), ALL, split_axis=0, concat_axis=0, tiled=True)

time: 47.2 us -> 40.5 us (0.86)
  Pallas kernels: 14.9 us -> 8.29 us
    pallas_call x1, Pallas kernels: 10.4 us -> 4.3 us  [owner_plan(): pl.pallas_call(functools.partial(cell_kernel, dims), out_shape=(jax.Shape...]
    pallas_call x1, Pallas kernels: 2.66 us -> 2.12 us  [owner_plan(): pl.pallas_call(functools.partial(pack_kernel, dims), out_shape=jax.ShapeD...]
where the time goes in v2:
time: 40.5 us; the launch traced here: 40.1 us
  blocking collectives  15.6 us (39%)
  waiting for transfers between devices  10.4 us (26%)
  Pallas kernels  8.29 us (20%)
  starting transfers between devices  2.59 us (6%)
  local copies, waits for them, and re-layouts  2.07 us (5%)
  between operations  0.96 us (2%)
    all_to_all x1, blocking collectives, owner_plan(): lax.all_to_all(packed.reshape(devices, rows, LANES), ALL, split_axis=0, c...  15.6 us
    all_to_all x1, waiting for transfers between devices, owner_plan(): lax.all_to_all(sent.reshape(devices, sent_rows, 1, LANES), ALL, split_axi...  10.4 us
    pallas_call x1, Pallas kernels, owner_plan(): pl.pallas_call(functools.partial(cell_kernel, dims), out_shape=(jax.Shape...  4.3 us
    all_to_all x1, starting transfers between devices, owner_plan(): lax.all_to_all(sent.reshape(devices, sent_rows, 1, LANES), ALL, split_axi...  2.59 us
    pallas_call x1, Pallas kernels, owner_plan(): pl.pallas_call(functools.partial(pack_kernel, dims), out_shape=jax.ShapeD...  2.12 us
    unnamed x22, local copies, waits for them, and re-layouts  2.07 us
    pallas_call x1, Pallas kernels, owner_plan(): pl.pallas_call(functools.partial(join_kernel, dims), out_shape=(jax.Shape...  1.87 us
  transfers between devices with their start and end apart: 1, of which 1 were waited for; matrix products, arithmetic and copies ran while one was open for 0% of the time, Pallas kernels for 0%

profile of v2, /device:TPU:0, one launch (start us, length us, event | category | flops | bytes accessed | tf_op | source)
XLA Modules:
  0.0 40.1 jit_solution(10298294909631780705)
XLA Ops:
  0.6 0.0 copy-start.5
  0.6 0.0 copy-start.9
  0.7 0.7 %copy-done.5 = s32[2048]{0:T(1024)S(1)} copy-done((s32[2048]{0:T(1024)S(1)}, s32[2048]{0:T(1024)}, u32[]{:S(2)}) %copy-start.5) | copy-done | bytes 8216
  1.3 0.0 copy-done.9
  1.3 2.1 %pack.1 = f32[256,128]{1,0:T(8,128)} custom-call(s32[8]{0:T(128)S(1)} %bitcast.128, f32[1,2048]{1,0:T(1,128)} %bitcast.123, s32[1,2048]{1,0:T(1,128)S(1)} %bitcast.120, s32[1,2048]{1,0:T(1,128)} %bitcast.121, s32[1,2048]{1,0:T(1,128)} %bitcast.122, f32[30,256]{1,0:T(8,128)} %a_ref.1, f32[30,256]{1,0:T(8,128)} %b_ref.1, f32[30,256]{1,0:T(8,128)} %c_ref.1, ...), custom_call_target="tpu_custom_call" | custom-call | tf_op jit(solution)/shard_map/pack/pallas_call | solution.py:379
  3.5 15.6 %all_to_all.43 = f32[32,8,128]{2,1,0:T(8,128)} all-to-all(f32[32,8,128]{2,1,0:T(8,128)} %bitcast.113), channel_id=1, replica_groups=mesh['geo'=8,'rep'=4] {'geo','rep'}, dimensions={0} | all-to-all | bytes 262144 | tf_op jit(solution)/shard_map/all_to_all | solution.py:386
  19.1 4.3 %cell.1 = (f32[544,128]{1,0:T(8,128)}, f32[1,128]{1,0:T(1,128)}) custom-call(f32[256,128]{1,0:T(8,128)} %bitcast.112), custom_call_target="tpu_custom_call" | custom-call | tf_op jit(solution)/shard_map/cell/pallas_call | solution.py:387
  23.4 2.6 %all-to-all-start.6 = ((f32[32,17,1,128]{3,2,1,0:T(1,128)}), f32[32,17,1,128]{3,2,1,0:T(1,128)S(1)}, u32[]{:S(2)}, u32[]{:S(2)}) async-start(f32[32,17,1,128]{3,2,1,0:T(1,128)} %bitcast.119), calls=%async_computation.6 | async-start | bytes 557056 | tf_op jit(solution)/shard_map/all_to_all | solution.py:404
  26.0 0.0 copy-start.10
  26.0 0.6 %copy-done.10 = f32[1,128]{1,0:T(1,128)S(1)} copy-done((f32[1,128]{1,0:T(1,128)S(1)}, f32[1,128]{1,0:T(1,128)}, u32[]{:S(2)}) %copy-start.10) | copy-done | bytes 536
  26.7 10.4 %all-to-all-done.6 = f32[32,17,1,128]{3,2,1,0:T(1,128)S(1)} async-done(((f32[32,17,1,128]{3,2,1,0:T(1,128)}), f32[32,17,1,128]{3,2,1,0:T(1,128)S(1)}, u32[]{:S(2)}, u32[]{:S(2)}) %all-to-all-start.6) | async-done | bytes 278560 | tf_op jit(solution)/shard_map/all_to_all | solution.py:404
  37.1 0.0 copy-start
  37.1 0.7 %copy-done = f32[32,17,1,128]{3,2,1,0:T(1,128)} copy-done((f32[32,17,1,128]{3,2,1,0:T(1,128)}, f32[32,17,1,128]{3,2,1,0:T(1,128)S(1)}, u32[]{:S(2)}) %copy-start) | copy-done | bytes 278552
  37.8 0.0 copy-start.1
  37.8 0.0 copy-start.2
  37.8 0.0 copy-start.3
  37.8 0.0 copy-start.4
  37.8 0.0 copy-start.6
  37.8 0.0 copy-start.7
  37.8 0.0 copy-start.8
  37.8 1.9 %join.1 = (f32[30,256]{1,0:T(8,128)}, f32[30,256]{1,0:T(8,128)}, f32[30,256]{1,0:T(8,128)}, f32[30,256]{1,0:T(8,128)}) custom-call(f32[544,128]{1,0:T(8,128)} %bitcast.108), custom_call_target="tpu_custom_call" | custom-call | tf_op jit(solution)/shard_map/join/pallas_call | solution.py:405
  39.7 0.0 copy-done.1
  39.7 0.0 copy-done.2
  39.7 0.0 copy-done.3
  39.7 0.0 copy-done.4
  39.7 0.0 copy-done.6
  39.7 0.0 copy-done.7
  39.7 0.0 copy-done.8
  39.7 0.2 conditional.1
Async XLA Ops:
  0.6 0.7 %copy-start.5 = (s32[2048]{0:T(1024)S(1)}, s32[2048]{0:T(1024)}, u32[]{:S(2)}) copy-start(s32[2048]{0:T(1024)} %param.16) | copy-start | bytes 24580
  0.6 0.7 %copy-start.9 = (s32[1,8,1]{1,2,0:T(1,128)S(1)}, s32[1,8,1]{1,2,0:T(1,128)}, u32[]{:S(2)}) copy-start(s32[1,8,1]{1,2,0:T(1,128)} %param.19) | copy-start | bytes 100
  23.4 13.7 %all-to-all-start.6 = ((f32[32,17,1,128]{3,2,1,0:T(1,128)}), f32[32,17,1,128]{3,2,1,0:T(1,128)S(1)}, u32[]{:S(2)}, u32[]{:S(2)}) async-start(f32[32,17,1,128]{3,2,1,0:T(1,128)} %bitcast.119), calls=%async_computation.6 | async-start | bytes 557056 | tf_op jit(solution)/shard_map/all_to_all | solution.py:404
  26.0 0.7 %copy-start.10 = (f32[1,128]{1,0:T(1,128)S(1)}, f32[1,128]{1,0:T(1,128)}, u32[]{:S(2)}) copy-start(f32[1,128]{1,0:T(1,128)} %get-tuple-element.112) | copy-start | bytes 1540
  37.1 0.7 %copy-start = (f32[32,17,1,128]{3,2,1,0:T(1,128)}, f32[32,17,1,128]{3,2,1,0:T(1,128)S(1)}, u32[]{:S(2)}) copy-start(f32[32,17,1,128]{3,2,1,0:T(1,128)S(1)} %all-to-all-done.6) | copy-start | bytes 835588
  37.8 1.9 %copy-start.1 = (f32[30,256]{1,0:T(8,128)S(1)}, f32[30,256]{1,0:T(8,128)}, u32[]{:S(2)}) copy-start(f32[30,256]{1,0:T(8,128)} %b_ref.1) | copy-start | bytes 92164
  37.8 1.9 %copy-start.2 = (f32[30,256]{1,0:T(8,128)S(1)}, f32[30,256]{1,0:T(8,128)}, u32[]{:S(2)}) copy-start(f32[30,256]{1,0:T(8,128)} %a_ref.1) | copy-start | bytes 92164
  37.8 1.9 %copy-start.3 = (f32[30,256]{1,0:T(8,128)S(1)}, f32[30,256]{1,0:T(8,128)}, u32[]{:S(2)}) copy-start(f32[30,256]{1,0:T(8,128)} %c_ref.1) | copy-start | bytes 92164
  37.8 1.9 %copy-start.4 = (f32[30,256]{1,0:T(8,128)S(1)}, f32[30,256]{1,0:T(8,128)}, u32[]{:S(2)}) copy-start(f32[30,256]{1,0:T(8,128)} %d_ref.1) | copy-start | bytes 92164
  37.8 1.9 %copy-start.6 = (s32[2048]{0:T(1024)S(1)}, s32[2048]{0:T(1024)}, u32[]{:S(2)}) copy-start(s32[2048]{0:T(1024)} %param.17) | copy-start | bytes 24580
  37.8 1.9 %copy-start.7 = (s32[2048]{0:T(1024)S(1)}, s32[2048]{0:T(1024)}, u32[]{:S(2)}) copy-start(s32[2048]{0:T(1024)} %param.18) | copy-start | bytes 24580
  37.8 1.9 %copy-start.8 = (f32[2048]{0:T(1024)S(1)}, f32[2048]{0:T(1024)}, u32[]{:S(2)}) copy-start(f32[2048]{0:T(1024)} %param.15) | copy-start | bytes 24580

commit v3 on v2

--- a/solution.py
+++ b/solution.py
@@ -141,19 +141,16 @@
     for at in range(0, tracts, LANES):
         put(row, mine[:, at : at + LANES])
         row += 1
-    owner = lax.broadcasted_iota(jnp.int32, (devices, listed * BLK), 1) // BLK
-    wanted = jnp.zeros((devices, listed * BLK), F32)
+    lane = lax.broadcasted_iota(jnp.int32, (devices, LANES), 1)
+    head = jnp.broadcast_to(largest, (devices, LANES))
     for p in range(listed):
-        wanted = jnp.where(owner == p, needed_ref[p].astype(F32), wanted)
-    for at in range(0, listed * BLK, LANES):
-        put(row, wanted[:, at : at + LANES])
-        row += 1
-    put(row, jnp.broadcast_to(largest, (devices, LANES)))
+        head = jnp.where(lane == p, needed_ref[p].astype(F32), head)
+    put(row, head)
 
 
 def cell_kernel(dims, in_ref, out_ref, flag_ref, pick_ref, mask_ref, weight_ref, hot_ref, turn_ref):
     rows, groups, reps, sent_rows = (dims[k] for k in ("rows", "groups", "reps", "sent_rows"))
-    at_res, at_slot, at_base, at_own, at_need, at_most = 0, 1, 2, 3, 5, 7
+    at_res, at_slot, at_base, at_own, at_head = 0, 1, 2, 3, 5
     tile = (groups, LANES)
     sub = lax.broadcasted_iota(jnp.int32, tile, 0)
     segment = lax.broadcasted_iota(jnp.int32, tile, 1) // BLK
@@ -182,7 +179,11 @@
         res, work = turned(unfold(at_own, res_rep, 0), slot), unfold(at_own, work_rep, 1)
         return [jnp.where(segment == 0, x, jnp.where(segment == 1, y, 0.0)) for x, y in zip(res, work)]
 
-    need = [jnp.where(segment == 1, x, -1.0) for x in turned(unfold(at_need, 0, 1), 0)]
+    lane = lax.broadcasted_iota(jnp.int32, tile, 1)
+    need = []
+    for g in range(groups):
+        own = jnp.sum(jnp.where(lane == sub, row_of(at_head, g * reps), 0.0), axis=1, keepdims=True)
+        need.append(jnp.where(segment == 1, own, -1.0))
 
     def fetch(v):
         tables = []
@@ -220,9 +221,8 @@
             columns = []
             for r in range(reps):
                 device = g * reps + r
-                mask = mask_ref[device]
-                parts = [jnp.concatenate([x.astype(F32)] * 2, axis=0) * mask for x in split3(values[device])]
-                columns.append(jnp.concatenate(parts, axis=0).astype(BF16))
+                mask = mask_ref[device].astype(BF16)
+                columns.append(jnp.concatenate([jnp.concatenate([x] * 2, axis=0) * mask for x in split3(values[device])], axis=0))
             sums = dot_nt(jnp.concatenate(columns, axis=1), hot_ref[g])
             sums = sums[: 2 * groups] + sums[2 * groups : 4 * groups] + sums[4 * groups :]
             sums = jnp.concatenate([sums, empty], axis=1)
@@ -231,13 +231,13 @@
                 folded[b] = folded[b] + jnp.where(need[g] == float(b), sums[groups:], 0.0)
         return [x + y for x, y in zip(res, folded)]
 
-    lam = fetch(both(0, 1, 1))
+    lam = fetch(both(0, 1, 0))
     weights = []
     for device in range(groups * reps):
         weight = row_of(at_base, device) * jnp.exp(along(device, lam[device // reps]))
         weight_ref[device] = weight
         weights.append(weight)
-    resid = [x - y for x, y in zip(both(2, 3, 2), scatter(weights))]
+    resid = [x - y for x, y in zip(both(2, 3, 1), scatter(weights))]
 
     def apply(v):
         tables = fetch(v)
@@ -275,19 +275,19 @@
             out_ref[pl.ds(r * sent_rows + row, groups, stride=reps * sent_rows), :] = value
 
     for k, v in enumerate(basis):
-        for part, tiles in enumerate((turned(v, 3 + k), v)):
+        for part, tiles in enumerate((turned(v, 2 + k), v)):
             for half in range(groups // side):
                 row = jnp.zeros(tile, F32)
                 for q in range(side):
                     row = jnp.where(segment == q, shifted(tiles[half * side + q], q - part), row)
                 put((2 * k + part) * (groups // side) + half, row)
-    lane = lax.broadcasted_iota(jnp.int32, tile, 1)
     numbers = jnp.zeros(tile, F32)
     for k, entry in enumerate(entries):
         numbers = jnp.where(lane == k, entry, numbers)
     put(sent_rows - 1, numbers)
-    most = in_ref[pl.ds(at_most, groups * reps, stride=rows), :]
-    flag_ref[...] = jnp.max(most, axis=0, keepdims=True)
+    most = in_ref[pl.ds(at_head, groups * reps, stride=rows), :]
+    most = jnp.max(most, axis=0, keepdims=True)
+    flag_ref[...] = jnp.broadcast_to(most[:, LANES - 1 :], (1, LANES))
 
 
 def join_kernel(dims, in_ref, step_res_ref, step_work_ref, resid_res_ref, resid_work_ref):
@@ -346,7 +346,7 @@
     slots = listed * BLK
     jobs = shapes["jobs"]
     cap = round_up(max(1, 3 * jobs // (2 * cells)), LANES)
-    rows = 8
+    rows = 6
     fits = (
         groups * reps >= cells
         and reps == 4
@@ -375,20 +375,26 @@
     )
     vmem = pl.BlockSpec(memory_space=pltpu.VMEM)
     smem = pl.BlockSpec(memory_space=pltpu.SMEM)
-    flat = lambda x: x.reshape(1, -1)
+    flat = lambda x: in_hbm(x.reshape(1, -1))
+    in_hbm = lambda x: pltpu.with_memory_space_constraint(x, pltpu.HBM)
+    in_vmem = lambda x: pltpu.with_memory_space_constraint(x, pltpu.VMEM)
     packed = pl.pallas_call(
         functools.partial(pack_kernel, dims),
-        out_shape=jax.ShapeDtypeStruct((devices * rows, LANES), F32),
+        out_shape=pltpu.VMEM((devices * rows, LANES), F32),
         in_specs=[smem] + [vmem] * 8,
         out_specs=vmem,
         name="pack",
-    )(needed.reshape(-1), flat(base), flat(job_res), flat(job_slot), flat(job_cell), lam_res, lam_work, target_res, target_work)
-    arrived = lax.all_to_all(packed.reshape(devices, rows, LANES), ALL, split_axis=0, concat_axis=0, tiled=True)
+    )(
+        in_hbm(needed.reshape(-1)),
+        *map(flat, (base, job_res, job_slot, job_cell)),
+        *map(in_hbm, (lam_res, lam_work, target_res, target_work)),
+    )
+    arrived = lax.all_to_all(packed.reshape(devices, rows, 1, LANES), ALL, split_axis=0, concat_axis=0, tiled=True)
     sent, most = pl.pallas_call(
         functools.partial(cell_kernel, dims),
         out_shape=(
-            jax.ShapeDtypeStruct((devices * sent_rows, LANES), F32),
-            jax.ShapeDtypeStruct((1, LANES), F32),
+            pltpu.VMEM((devices * sent_rows, LANES), F32),
+            pltpu.VMEM((1, LANES), F32),
         ),
         in_specs=[vmem],
         out_specs=(vmem, vmem),
@@ -397,10 +403,11 @@
             pltpu.VMEM((devices, 2 * groups, LANES), F32),
             pltpu.VMEM((devices, groups, LANES), F32),
             pltpu.VMEM((groups, 2 * BLK, reps * LANES), BF16),
-            pltpu.VMEM((3 + ITERS + 1, groups * groups, LANES), F32),
+            pltpu.VMEM((2 + ITERS + 1, groups * groups, LANES), F32),
         ],
         name="cell",
-    )(arrived.reshape(devices * rows, LANES))
+    )(in_vmem(arrived.reshape(devices * rows, LANES)))
+    sent, over = lax.optimization_barrier((sent, (most[0, 0] > dims["cap"]).astype(jnp.int32)))
     back = lax.all_to_all(sent.reshape(devices, sent_rows, 1, LANES), ALL, split_axis=0, concat_axis=0, tiled=True)
     outs = pl.pallas_call(
         functools.partial(join_kernel, dims),
@@ -408,17 +415,24 @@
         in_specs=[vmem],
         out_specs=(vmem,) * 4,
         name="join",
-    )(back.reshape(devices * sent_rows, LANES))
-    return outs, most[0, 0] > dims["cap"]
+    )(in_vmem(back.reshape(devices * sent_rows, LANES)))
+    return outs, packed, over
 
 
 def body(mesh_shape, *args):
     base, needed, lam_res = args[0], args[4], args[5]
+    shape = needed.shape
     fits, dims = plan_dims(mesh_shape, {"lam": lam_res.shape, "needed": needed.shape, "jobs": base.shape[0]})
     if not fits:
         return start_plan(*args)
-    outs, over = owner_plan(dims, *args)
-    return lax.cond(over, lambda: tuple(start_plan(*args)), lambda: tuple(outs))
+    outs, head, over = owner_plan(dims, *args)
+    outs, head, over, args = lax.optimization_barrier((outs, head, over, args[:4] + args[5:]))
+
+    def other():
+        needed = head[dims["rows"] - 1, : dims["listed"]].astype(jnp.int32).reshape(shape)
+        return tuple(start_plan(*args[:4], needed, *args[4:]))
+
+    return lax.cond(over > 0, other, lambda: tuple(outs))
 
 
 def solution(mesh):

time: 40.5 us -> 34.1 us (0.84)
  blocking collectives: 15.6 us -> 27.7 us
  waiting for transfers between devices: 10.4 us -> 0 us
  Pallas kernels: 8.29 us -> 4.99 us
  starting transfers between devices: 2.59 us -> 0 us
  local copies, waits for them, and re-layouts: 2.07 us -> 0.04 us
    all_to_all x1 -> x2, blocking collectives: 15.6 us -> 27.7 us  [the longest x1 14.9 us: owner_plan(): lax.all_to_all(packed.reshape(devices, rows, 1, LANES), ALL, split_axis=0...]
    all_to_all x1 -> x0, waiting for transfers between devices: 10.4 us -> none  [owner_plan(): lax.all_to_all(sent.reshape(devices, sent_rows, 1, LANES), ALL, split_axi...]
    all_to_all x1 -> x0, starting transfers between devices: 2.59 us -> none  [owner_plan(): lax.all_to_all(sent.reshape(devices, sent_rows, 1, LANES), ALL, split_axi...]
    pallas_call x2, Pallas kernels: 6.42 us -> 4.13 us  [the longest x1 2.64 us: owner_plan(): pl.pallas_call(functools.partial(cell_kernel, dims), out_shape=(pltpu.VME...]
    unnamed x22 -> x16, local copies, waits for them, and re-layouts: 2.07 us -> 0.04 us
    pallas_call x1, Pallas kernels: 1.87 us -> 0.85 us  [owner_plan(): pl.pallas_call(functools.partial(join_kernel, dims), out_shape=(jax.Shape...]
  transfers between devices with their start and end apart: 1 -> 0, of which waited for: 1 -> 0; matrix products, arithmetic and copies ran while one was open for 0% -> 0% of each run, Pallas kernels for 0% -> 0%
where the time goes in v3:
time: 34.1 us; the launch traced here: 33.9 us
  blocking collectives  27.7 us (81%)
  Pallas kernels  4.99 us (15%)
  between operations  0.95 us (3%)
    all_to_all x1, blocking collectives, owner_plan(): lax.all_to_all(packed.reshape(devices, rows, 1, LANES), ALL, split_axis=0...  14.9 us
    all_to_all x1, blocking collectives, owner_plan(): lax.all_to_all(sent.reshape(devices, sent_rows, 1, LANES), ALL, split_axi...  12.8 us
    pallas_call x1, Pallas kernels, owner_plan(): pl.pallas_call(functools.partial(cell_kernel, dims), out_shape=(pltpu.VME...  2.64 us
    pallas_call x1, Pallas kernels, owner_plan(): pl.pallas_call(functools.partial(pack_kernel, dims), out_shape=pltpu.VMEM...  1.5 us
    pallas_call x1, Pallas kernels, owner_plan(): pl.pallas_call(functools.partial(join_kernel, dims), out_shape=(jax.Shape...  0.85 us

profile of v3, /device:TPU:0, one launch (start us, length us, event | category | flops | bytes accessed | tf_op | source)
XLA Modules:
  0.0 33.9 jit_solution(14987015294108108597)
XLA Ops:
  0.6 1.5 %pack.1 = f32[192,128]{1,0:T(8,128)S(1)} custom-call(s32[8]{0:T(128)} %bitcast.130, f32[1,2048]{1,0:T(1,128)} %bitcast.125, s32[1,2048]{1,0:T(1,128)} %bitcast.122, s32[1,2048]{1,0:T(1,128)} %bitcast.123, s32[1,2048]{1,0:T(1,128)} %bitcast.124, f32[30,256]{1,0:T(8,128)} %a_ref.1, f32[30,256]{1,0:T(8,128)} %b_ref.1, f32[30,256]{1,0:T(8,128)} %c_ref.1, ...), custom_call_target="tpu_custom_call" | custom-call | tf_op jit(solution)/shard_map/pack/pallas_call | solution.py:381
  2.1 14.9 %all_to_all.41 = f32[32,6,1,128]{3,2,1,0:T(1,128)S(1)} all-to-all(f32[32,6,1,128]{3,2,1,0:T(1,128)S(1)} %bitcast.107), channel_id=1, replica_groups=mesh['geo'=8,'rep'=4] {'geo','rep'}, dimensions={0} | all-to-all | bytes 196608 | tf_op jit(solution)/shard_map/all_to_all | solution.py:392
  17.0 2.6 %cell.1 = (f32[544,128]{1,0:T(8,128)S(1)}, f32[1,128]{1,0:T(1,128)S(1)}) custom-call(f32[192,128]{1,0:T(8,128)S(1)} %bitcast.106), custom_call_target="tpu_custom_call" | custom-call | tf_op jit(solution)/shard_map/cell/pallas_call | solution.py:393
  19.7 12.8 %all_to_all.42 = f32[32,17,1,128]{3,2,1,0:T(1,128)S(1)} all-to-all(f32[32,17,1,128]{3,2,1,0:T(1,128)S(1)} %bitcast.108), channel_id=1, replica_groups=mesh['geo'=8,'rep'=4] {'geo','rep'}, dimensions={0} | all-to-all | bytes 557056 | tf_op jit(solution)/shard_map/all_to_all | solution.py:411
  32.5 0.0 copy-start
  32.5 0.0 copy-start.1
  32.5 0.0 copy-start.2
  32.5 0.0 copy-start.3
  32.5 0.0 copy-start.4
  32.5 0.0 copy-start.5
  32.6 0.0 copy-start.6
  32.6 0.0 copy-start.7
  32.6 0.9 %join.1 = (f32[30,256]{1,0:T(8,128)}, f32[30,256]{1,0:T(8,128)}, f32[30,256]{1,0:T(8,128)}, f32[30,256]{1,0:T(8,128)}) custom-call(f32[544,128]{1,0:T(8,128)S(1)} %bitcast.105), custom_call_target="tpu_custom_call" | custom-call | tf_op jit(solution)/shard_map/join/pallas_call | solution.py:412
  33.4 0.0 copy-done
  33.4 0.0 copy-done.1
  33.4 0.0 copy-done.2
  33.4 0.0 copy-done.3
  33.5 0.0 copy-done.4
  33.5 0.0 copy-done.5
  33.5 0.0 copy-done.6
  33.5 0.0 copy-done.7
  33.5 0.2 conditional.1
Async XLA Ops:
  32.5 0.9 %copy-start = (f32[30,256]{1,0:T(8,128)S(1)}, f32[30,256]{1,0:T(8,128)}, u32[]{:S(2)}) copy-start(f32[30,256]{1,0:T(8,128)} %b_ref.1) | copy-start | bytes 92164
  32.5 0.9 %copy-start.1 = (f32[30,256]{1,0:T(8,128)S(1)}, f32[30,256]{1,0:T(8,128)}, u32[]{:S(2)}) copy-start(f32[30,256]{1,0:T(8,128)} %a_ref.1) | copy-start | bytes 92164
  32.5 0.9 %copy-start.2 = (f32[30,256]{1,0:T(8,128)S(1)}, f32[30,256]{1,0:T(8,128)}, u32[]{:S(2)}) copy-start(f32[30,256]{1,0:T(8,128)} %c_ref.1) | copy-start | bytes 92164
  32.5 0.9 %copy-start.3 = (f32[30,256]{1,0:T(8,128)S(1)}, f32[30,256]{1,0:T(8,128)}, u32[]{:S(2)}) copy-start(f32[30,256]{1,0:T(8,128)} %d_ref.1) | copy-start | bytes 92164
  32.5 0.9 %copy-start.4 = (s32[2048]{0:T(1024)S(1)}, s32[2048]{0:T(1024)}, u32[]{:S(2)}) copy-start(s32[2048]{0:T(1024)} %param.16) | copy-start | bytes 24580
  32.5 0.9 %copy-start.5 = (s32[2048]{0:T(1024)S(1)}, s32[2048]{0:T(1024)}, u32[]{:S(2)}) copy-start(s32[2048]{0:T(1024)} %param.17) | copy-start | bytes 24580
  32.6 0.9 %copy-start.6 = (s32[2048]{0:T(1024)S(1)}, s32[2048]{0:T(1024)}, u32[]{:S(2)}) copy-start(s32[2048]{0:T(1024)} %param.18) | copy-start | bytes 24580
  32.6 0.9 %copy-start.7 = (f32[2048]{0:T(1024)S(1)}, f32[2048]{0:T(1024)}, u32[]{:S(2)}) copy-start(f32[2048]{0:T(1024)} %param.15) | copy-start | bytes 24580

commit v4 on v3

--- a/solution.py
+++ b/solution.py
@@ -11,6 +11,7 @@
 ITERS = 3
 RIDGE = 0.5
 LANES = 128
+HALVES = 2
 ALL = ("geo", "rep")
 
 F32 = jnp.float32
@@ -270,8 +271,8 @@
         entries += [middle, off]
         basis.append(v)
 
-    def put(row, value):
-        for r in range(reps):
+    def put(row, value, which):
+        for r in which:
             out_ref[pl.ds(r * sent_rows + row, groups, stride=reps * sent_rows), :] = value
 
     for k, v in enumerate(basis):
@@ -280,18 +281,18 @@
                 row = jnp.zeros(tile, F32)
                 for q in range(side):
                     row = jnp.where(segment == q, shifted(tiles[half * side + q], q - part), row)
-                put((2 * k + part) * (groups // side) + half, row)
+                put(2 * k + part, row, range(half, reps, HALVES))
     numbers = jnp.zeros(tile, F32)
     for k, entry in enumerate(entries):
         numbers = jnp.where(lane == k, entry, numbers)
-    put(sent_rows - 1, numbers)
+    put(sent_rows - 1, numbers, range(reps))
     most = in_ref[pl.ds(at_head, groups * reps, stride=rows), :]
     most = jnp.max(most, axis=0, keepdims=True)
     flag_ref[...] = jnp.broadcast_to(most[:, LANES - 1 :], (1, LANES))
 
 
-def join_kernel(dims, in_ref, step_res_ref, step_work_ref, resid_res_ref, resid_work_ref):
-    devices, sent_rows, groups, cells = dims["devices"], dims["sent_rows"], dims["groups"], dims["cells"]
+def join_kernel(dims, in_ref, out_ref):
+    devices, sent_rows = dims["devices"], dims["sent_rows"]
     tile = (devices, LANES)
 
     def take(row):
@@ -326,13 +327,19 @@
         direct = [r + beta * d for r, d in zip(resid, direct)] + resid[len(direct) :]
         norm = following
 
-    half = groups * BLK // LANES
-    for part, (step_ref, resid_ref) in enumerate(((step_res_ref, resid_res_ref), (step_work_ref, resid_work_ref))):
-        for at in range(half):
-            vectors = [take((2 * k + part) * half + at) for k in range(ITERS + 1)]
-            lanes = slice(at * LANES, (at + 1) * LANES)
-            step_ref[:, lanes] = sum(s * v for s, v in zip(step, vectors))[:cells]
-            resid_ref[:, lanes] = sum(r * v for r, v in zip(resid, vectors))[:cells]
+    for part in range(2):
+        vectors = [take(2 * k + part) for k in range(ITERS + 1)]
+        out_ref[pl.ds(part * devices, devices), :] = sum(s * v for s, v in zip(step, vectors))
+        out_ref[pl.ds((2 + part) * devices, devices), :] = sum(r * v for r, v in zip(resid, vectors))
+
+
+def place_kernel(dims, own_ref, other_ref, *out_refs):
+    devices, cells = dims["devices"], dims["cells"]
+    first = lax.axis_index("rep") % HALVES == 0
+    for k, out_ref in enumerate(out_refs):
+        own, other = own_ref[pl.ds(k * devices, devices), :], other_ref[pl.ds(k * devices, devices), :]
+        out_ref[:, :LANES] = jnp.where(first, own, other)[:cells]
+        out_ref[:, LANES:] = jnp.where(first, other, own)[:cells]
 
 
 def round_up(value, unit):
@@ -352,7 +359,7 @@
         and reps == 4
         and groups == 8
         and listed == groups
-        and tracts == groups * BLK
+        and tracts == groups * BLK == HALVES * LANES
         and cap == LANES
         and jobs % 256 == 0
     )
@@ -365,7 +372,7 @@
         listed=listed,
         cap=cap,
         rows=rows,
-        sent_rows=2 * groups + 1,
+        sent_rows=2 * (ITERS + 1) + 1,
     )
 
 
@@ -409,13 +416,21 @@
     )(in_vmem(arrived.reshape(devices * rows, LANES)))
     sent, over = lax.optimization_barrier((sent, (most[0, 0] > dims["cap"]).astype(jnp.int32)))
     back = lax.all_to_all(sent.reshape(devices, sent_rows, 1, LANES), ALL, split_axis=0, concat_axis=0, tiled=True)
-    outs = pl.pallas_call(
+    own = pl.pallas_call(
         functools.partial(join_kernel, dims),
-        out_shape=(jax.ShapeDtypeStruct((cells, tracts), F32),) * 4,
+        out_shape=pltpu.VMEM((4 * devices, LANES), F32),
         in_specs=[vmem],
-        out_specs=(vmem,) * 4,
+        out_specs=vmem,
         name="join",
     )(in_vmem(back.reshape(devices * sent_rows, LANES)))
+    other = lax.ppermute(own, "rep", [(r, r ^ 1) for r in range(reps)])
+    outs = pl.pallas_call(
+        functools.partial(place_kernel, dims),
+        out_shape=(jax.ShapeDtypeStruct((cells, tracts), F32),) * 4,
+        in_specs=[vmem] * 2,
+        out_specs=(vmem,) * 4,
+        name="place",
+    )(in_vmem(own), in_vmem(other))
     return outs, packed, over
 
 

time: 34.1 us -> 32.8 us (0.962)
  blocking collectives: 27.7 us -> 25 us
  waiting for transfers between devices: 0 us -> 0.99 us
    all_to_all x1, blocking collectives: 12.8 us -> 10.1 us  [owner_plan(): lax.all_to_all(sent.reshape(devices, sent_rows, 1, LANES), ALL, split_axi...]
    ppermute x0 -> x1, waiting for transfers between devices: none -> 0.99 us  [owner_plan(): other = lax.ppermute(own, 'rep', [(r, r ^ 1) for r in range(reps)])]
    pallas_call x1 -> x2, Pallas kernels: 0.85 us -> 0.85 us  [the longest x1 0.66 us: owner_plan(): pl.pallas_call(functools.partial(place_kernel, dims), out_shape=(jax.Shap...]
  transfers between devices with their start and end apart: 0 -> 1, of which waited for: 0 -> 1; matrix products, arithmetic and copies ran while one was open for 0% -> 0% of each run, Pallas kernels for 0% -> 0%
where the time goes in v4:
time: 32.8 us; the launch traced here: 32.6 us
  blocking collectives  25 us (76%)
  Pallas kernels  4.99 us (15%)
  waiting for transfers between devices  0.99 us (3%)
  between operations  0.95 us (3%)
  starting transfers between devices  0.33 us (1%)
    all_to_all x1, blocking collectives, owner_plan(): lax.all_to_all(packed.reshape(devices, rows, 1, LANES), ALL, split_axis=0...  14.9 us
    all_to_all x1, blocking collectives, owner_plan(): lax.all_to_all(sent.reshape(devices, sent_rows, 1, LANES), ALL, split_axi...  10.1 us
    pallas_call x1, Pallas kernels, owner_plan(): pl.pallas_call(functools.partial(cell_kernel, dims), out_shape=(pltpu.VME...  2.64 us
    pallas_call x1, Pallas kernels, owner_plan(): pl.pallas_call(functools.partial(pack_kernel, dims), out_shape=pltpu.VMEM...  1.5 us
    ppermute x1, waiting for transfers between devices, owner_plan(): other = lax.ppermute(own, 'rep', [(r, r ^ 1) for r in range(reps)])  0.99 us
    pallas_call x1, Pallas kernels, owner_plan(): pl.pallas_call(functools.partial(place_kernel, dims), out_shape=(jax.Shap...  0.66 us
  transfers between devices with their start and end apart: 1, of which 1 were waited for; matrix products, arithmetic and copies ran while one was open for 0% of the time, Pallas kernels for 0%

profile of v4, /device:TPU:0, one launch (start us, length us, event | category | flops | bytes accessed | tf_op | source)
XLA Modules:
  0.0 32.6 jit_solution(8247852440547009160)
XLA Ops:
  0.6 1.5 %pack.1 = f32[192,128]{1,0:T(8,128)S(1)} custom-call(s32[8]{0:T(128)} %bitcast.130, f32[1,2048]{1,0:T(1,128)} %bitcast.125, s32[1,2048]{1,0:T(1,128)} %bitcast.122, s32[1,2048]{1,0:T(1,128)} %bitcast.123, s32[1,2048]{1,0:T(1,128)} %bitcast.124, f32[30,256]{1,0:T(8,128)} %a_ref.1, f32[30,256]{1,0:T(8,128)} %b_ref.1, f32[30,256]{1,0:T(8,128)} %c_ref.1, ...), custom_call_target="tpu_custom_call" | custom-call | tf_op jit(solution)/shard_map/pack/pallas_call | solution.py:388
  2.1 14.9 %all_to_all.41 = f32[32,6,1,128]{3,2,1,0:T(1,128)S(1)} all-to-all(f32[32,6,1,128]{3,2,1,0:T(1,128)S(1)} %bitcast.107), channel_id=1, replica_groups=mesh['geo'=8,'rep'=4] {'geo','rep'}, dimensions={0} | all-to-all | bytes 196608 | tf_op jit(solution)/shard_map/all_to_all | solution.py:399
  17.0 2.6 %cell.1 = (f32[288,128]{1,0:T(8,128)S(1)}, f32[1,128]{1,0:T(1,128)S(1)}) custom-call(f32[192,128]{1,0:T(8,128)S(1)} %bitcast.106), custom_call_target="tpu_custom_call" | custom-call | tf_op jit(solution)/shard_map/cell/pallas_call | solution.py:400
  19.7 10.1 %all_to_all.42 = f32[32,9,1,128]{3,2,1,0:T(1,128)S(1)} all-to-all(f32[32,9,1,128]{3,2,1,0:T(1,128)S(1)} %bitcast.108), channel_id=1, replica_groups=mesh['geo'=8,'rep'=4] {'geo','rep'}, dimensions={0} | all-to-all | bytes 294912 | tf_op jit(solution)/shard_map/all_to_all | solution.py:418
  29.9 0.0 copy-start.4
  29.9 0.0 copy-start.5
  29.9 0.0 copy-start.6
  29.9 0.0 copy-start.7
  29.9 0.2 join.1.own_ref
  30.1 0.0 copy-start
  30.1 0.0 copy-start.1
  30.1 0.0 copy-start.2
  30.1 0.0 copy-start.3
  30.1 0.3 %collective-permute-start = (f32[128,128]{1,0:T(8,128)S(1)}, f32[128,128]{1,0:T(8,128)S(1)}, u32[]{:S(2)}, u32[]{:S(2)}) collective-permute-start(f32[128,128]{1,0:T(8,128)S(1)} %join.1.own_ref), channel_id=1, source_target_pairs={{0,1},{1,0},{2,3},{3,2},{4,5},{5,4},{6,7},{7,6},{8,9},{9,8},{10,11... | collective-permute-start | bytes 196616 | tf_op jit(solution)/shard_map/ppermute | solution.py:426
  30.4 1.0 %collective-permute-done.other_ref = f32[128,128]{1,0:T(8,128)S(1)} collective-permute-done((f32[128,128]{1,0:T(8,128)S(1)}, f32[128,128]{1,0:T(8,128)S(1)}, u32[]{:S(2)}, u32[]{:S(2)}) %collective-permute-start) | collective-permute-done | bytes 65568 | tf_op jit(solution)/shard_map/ppermute | solution.py:426
  31.4 0.7 %place.1 = (f32[30,256]{1,0:T(8,128)}, f32[30,256]{1,0:T(8,128)}, f32[30,256]{1,0:T(8,128)}, f32[30,256]{1,0:T(8,128)}) custom-call(f32[128,128]{1,0:T(8,128)S(1)} %join.1.own_ref, f32[128,128]{1,0:T(8,128)S(1)} %collective-permute-done.other_ref), custom_call_target="tpu_custom_call" | custom-call | tf_op jit(solution)/shard_map/place/pallas_call | solution.py:427
  32.1 0.0 copy-done.4
  32.1 0.0 copy-done.5
  32.1 0.0 copy-done.6
  32.1 0.0 copy-done.7
  32.1 0.0 copy-done
  32.1 0.0 copy-done.1
  32.1 0.0 copy-done.2
  32.1 0.0 copy-done.3
  32.2 0.2 conditional.1
Async XLA Ops:
  29.9 2.2 %copy-start.4 = (s32[2048]{0:T(1024)S(1)}, s32[2048]{0:T(1024)}, u32[]{:S(2)}) copy-start(s32[2048]{0:T(1024)} %param.16) | copy-start | bytes 24580
  29.9 2.2 %copy-start.5 = (s32[2048]{0:T(1024)S(1)}, s32[2048]{0:T(1024)}, u32[]{:S(2)}) copy-start(s32[2048]{0:T(1024)} %param.17) | copy-start | bytes 24580
  29.9 2.2 %copy-start.6 = (s32[2048]{0:T(1024)S(1)}, s32[2048]{0:T(1024)}, u32[]{:S(2)}) copy-start(s32[2048]{0:T(1024)} %param.18) | copy-start | bytes 24580
  29.9 2.2 %copy-start.7 = (f32[2048]{0:T(1024)S(1)}, f32[2048]{0:T(1024)}, u32[]{:S(2)}) copy-start(f32[2048]{0:T(1024)} %param.15) | copy-start | bytes 24580
  30.1 2.0 %copy-start = (f32[30,256]{1,0:T(8,128)S(1)}, f32[30,256]{1,0:T(8,128)}, u32[]{:S(2)}) copy-start(f32[30,256]{1,0:T(8,128)} %b_ref.1) | copy-start | bytes 92164
  30.1 2.0 %copy-start.1 = (f32[30,256]{1,0:T(8,128)S(1)}, f32[30,256]{1,0:T(8,128)}, u32[]{:S(2)}) copy-start(f32[30,256]{1,0:T(8,128)} %a_ref.1) | copy-start | bytes 92164
  30.1 2.0 %copy-start.2 = (f32[30,256]{1,0:T(8,128)S(1)}, f32[30,256]{1,0:T(8,128)}, u32[]{:S(2)}) copy-start(f32[30,256]{1,0:T(8,128)} %c_ref.1) | copy-start | bytes 92164
  30.1 2.0 %copy-start.3 = (f32[30,256]{1,0:T(8,128)S(1)}, f32[30,256]{1,0:T(8,128)}, u32[]{:S(2)}) copy-start(f32[30,256]{1,0:T(8,128)} %d_ref.1) | copy-start | bytes 92164
  30.1 1.3 %collective-permute-start = (f32[128,128]{1,0:T(8,128)S(1)}, f32[128,128]{1,0:T(8,128)S(1)}, u32[]{:S(2)}, u32[]{:S(2)}) collective-permute-start(f32[128,128]{1,0:T(8,128)S(1)} %join.1.own_ref), channel_id=1, source_target_pairs={{0,1},{1,0},{2,3},{3,2},{4,5},{5,4},{6,7},{7,6},{8,9},{9,8},{10,11... | collective-permute-start | bytes 196616 | tf_op jit(solution)/shard_map/ppermute | solution.py:426

commit v5 on v4

--- a/solution.py
+++ b/solution.py
@@ -149,25 +149,25 @@
     put(row, head)
 
 
-def cell_kernel(dims, in_ref, out_ref, flag_ref, pick_ref, mask_ref, weight_ref, hot_ref, turn_ref):
+def cell_kernel(dims, in_ref, out_ref, flag_ref, digit_ref, mask_ref, hot_ref, part_ref, turn_ref):
     rows, groups, reps, sent_rows = (dims[k] for k in ("rows", "groups", "reps", "sent_rows"))
     at_res, at_slot, at_base, at_own, at_head = 0, 1, 2, 3, 5
     tile = (groups, LANES)
+    side = LANES // BLK
     sub = lax.broadcasted_iota(jnp.int32, tile, 0)
-    segment = lax.broadcasted_iota(jnp.int32, tile, 1) // BLK
-
-    side = LANES // BLK
-
-    def row_of(row, device):
-        return jnp.broadcast_to(in_ref[pl.ds(device * rows + row, 1), :], tile)
+    lane = lax.broadcasted_iota(jnp.int32, tile, 1)
+    segment = lane // BLK
+
+    def of_groups(row, rep):
+        return in_ref[pl.ds(rep * rows + row, groups, stride=reps * rows), :]
 
     def shifted(x, segments):
         return pltpu.roll(x, BLK * (segments % side), 1) if segments % side else x
 
-    def unfold(row, rep, place):
+    def unfold(rep, place):
         tiles = []
         for half in range(groups // side):
-            x = in_ref[pl.ds(rep * rows + row + half, groups, stride=reps * rows), :]
+            x = of_groups(at_own + half, rep)
             tiles += [shifted(x, place - k) for k in range(side)]
         return tiles
 
@@ -176,74 +176,80 @@
             turn_ref[slot, pl.ds(b, groups, stride=groups), :] = x
         return [turn_ref[slot, pl.ds(g * groups, groups), :] for g in range(groups)]
 
-    def both(res_rep, work_rep, slot):
-        res, work = turned(unfold(at_own, res_rep, 0), slot), unfold(at_own, work_rep, 1)
-        return [jnp.where(segment == 0, x, jnp.where(segment == 1, y, 0.0)) for x, y in zip(res, work)]
-
-    lane = lax.broadcasted_iota(jnp.int32, tile, 1)
+    head = of_groups(at_head, 0)
+    halves = range(groups // side)
+    choose = [jnp.take_along_axis(head, half * side + segment, axis=1).astype(jnp.int32) for half in halves]
     need = []
     for g in range(groups):
-        own = jnp.sum(jnp.where(lane == sub, row_of(at_head, g * reps), 0.0), axis=1, keepdims=True)
-        need.append(jnp.where(segment == 1, own, -1.0))
-
-    def fetch(v):
-        tables = []
-        for g in range(groups):
-            table = jnp.where(segment == 0, v[g], 0.0)
-            for b in range(groups):
-                table = jnp.where(need[g] == float(b), v[b], table)
-            tables.append(table)
-        return tables
-
-    low = lax.broadcasted_iota(jnp.int32, (BLK, LANES), 0)
+        row = jnp.broadcast_to(in_ref[pl.ds(g * reps * rows + at_head, 1), :], tile)
+        listed = jnp.sum(jnp.where(lane == sub, row, 0.0), axis=1, keepdims=True)
+        need.append(jnp.where(segment == 1, listed, -1.0))
+
+    tracts = [[of_groups(row, r).astype(jnp.int32) for r in range(reps)] for row in (at_res, at_slot)]
+    for kind in range(2):
+        for r, x in enumerate(tracts[kind]):
+            digit_ref[2 * kind, pl.ds(r * groups, groups), :] = (x & (BLK - 1)).astype(F32)
+            high = lax.shift_right_logical(x, BLK.bit_length() - 1)
+            digit_ref[2 * kind + 1, pl.ds(r * groups, groups), :] = high.astype(F32)
+
+    place = lax.broadcasted_iota(jnp.int32, (BLK, LANES), 0).astype(F32).astype(BF16)
+    sub_f = sub.astype(F32)
+    one, none = jnp.ones((BLK, LANES), BF16), jnp.zeros((BLK, LANES), BF16)
     for g in range(groups):
         for r in range(reps):
-            device = g * reps + r
-            res = row_of(at_res, device).astype(jnp.int32)
-            slot = row_of(at_slot, device).astype(jnp.int32)
-            pick_ref[device, :groups, :] = res % BLK
-            pick_ref[device, groups:, :] = slot % BLK + BLK
-            mask_ref[device, :groups, :] = (res // BLK == sub).astype(F32)
-            mask_ref[device, groups:, :] = (slot // BLK == sub).astype(F32)
             lanes = slice(r * LANES, (r + 1) * LANES)
-            hot_ref[g, :BLK, lanes] = (low == (res % BLK)[:1]).astype(F32).astype(BF16)
-            hot_ref[g, BLK:, lanes] = (low == (slot % BLK)[:1]).astype(F32).astype(BF16)
-
-    def along(device, table):
-        picked = jnp.take_along_axis(table, pick_ref[device, :groups, :], axis=1) * mask_ref[device, :groups, :]
-        picked += jnp.take_along_axis(table, pick_ref[device, groups:, :], axis=1) * mask_ref[device, groups:, :]
-        return jnp.broadcast_to(jnp.sum(picked, axis=0, keepdims=True), tile)
+            masks = []
+            for kind in range(2):
+                digit = lambda k: digit_ref[2 * kind + k, pl.ds(r * groups + g, 1), :]
+                masks.append((jnp.broadcast_to(digit(1), tile) == sub_f).astype(F32))
+                spot = jnp.broadcast_to(digit(0), (BLK, LANES)).astype(BF16)
+                hot_ref[g, kind * BLK : (kind + 1) * BLK, lanes] = jnp.where(spot == place, one, none)
+            mask_ref[g, :, lanes] = jnp.concatenate(masks, axis=0).astype(BF16)
+
+    def folded(tiles, place):
+        out = []
+        for half in halves:
+            x = shifted(tiles[half * side], -place)
+            for q in range(1, side):
+                x = jnp.where(segment == q, shifted(tiles[half * side + q], q - place), x)
+            out.append(x)
+        return out
+
+    def along(res, owned):
+        work = [jnp.take_along_axis(x, chosen, axis=0) for x, chosen in zip(owned, choose)]
+        out = []
+        for r in range(reps):
+            value = 0.0
+            for table, tract in ((res, tracts[0][r]), (work, tracts[1][r])):
+                spot = tract & (LANES - 1)
+                first, second = (jnp.take_along_axis(x, spot, axis=1) for x in table)
+                value += jnp.where(tract < LANES, first, second)
+            out.append(value)
+        return out
 
     empty = jnp.zeros((2 * groups, LANES - 2 * BLK), F32)
 
-    def scatter(values):
-        res, folded = [], [jnp.zeros(tile, F32)] * groups
+    def scatter(values, slot):
+        for r in range(reps):
+            for k, x in enumerate(split3(values[r])):
+                part_ref[slot, k, pl.ds(r * groups, groups), :] = x.astype(F32)
+        res, work = [], [jnp.zeros(tile, F32)] * groups
         for g in range(groups):
             columns = []
             for r in range(reps):
-                device = g * reps + r
-                mask = mask_ref[device].astype(BF16)
-                columns.append(jnp.concatenate([jnp.concatenate([x] * 2, axis=0) * mask for x in split3(values[device])], axis=0))
+                mask = mask_ref[g, :, r * LANES : (r + 1) * LANES]
+                parts = [
+                    jnp.broadcast_to(part_ref[slot, k, pl.ds(r * groups + g, 1), :], (2 * groups, LANES)).astype(BF16)
+                    for k in range(3)
+                ]
+                columns.append(jnp.concatenate([x * mask for x in parts], axis=0))
             sums = dot_nt(jnp.concatenate(columns, axis=1), hot_ref[g])
             sums = sums[: 2 * groups] + sums[2 * groups : 4 * groups] + sums[4 * groups :]
             sums = jnp.concatenate([sums, empty], axis=1)
             res.append(jnp.where(segment == 0, sums[:groups], 0.0))
             for b in range(groups):
-                folded[b] = folded[b] + jnp.where(need[g] == float(b), sums[groups:], 0.0)
-        return [x + y for x, y in zip(res, folded)]
-
-    lam = fetch(both(0, 1, 0))
-    weights = []
-    for device in range(groups * reps):
-        weight = row_of(at_base, device) * jnp.exp(along(device, lam[device // reps]))
-        weight_ref[device] = weight
-        weights.append(weight)
-    resid = [x - y for x, y in zip(both(2, 3, 1), scatter(weights))]
-
-    def apply(v):
-        tables = fetch(v)
-        image = scatter([weight_ref[device] * along(device, tables[device // reps]) for device in range(groups * reps)])
-        return [x + RIDGE * y for x, y in zip(image, v)]
+                work[b] = work[b] + jnp.where(need[g] == float(b), sums[groups:], 0.0)
+        return [x + y for x, y in zip(res, work)]
 
     def dot(a, b):
         products = [x * y for x, y in zip(a, b)]
@@ -251,39 +257,58 @@
             products = [x + y for x, y in zip(products[::2], products[1::2])]
         return jnp.sum(jnp.sum(products[0], axis=0, keepdims=True), axis=1, keepdims=True)
 
-    def unit(w):
-        square = dot(w, w)
-        some = square > 0.0
-        scale = jnp.where(some, lax.rsqrt(jnp.where(some, square, 1.0)), 0.0)
-        return square * scale, [x * scale for x in w]
-
-    size, v = unit(resid)
-    basis, entries = [v], [size]
-    last, off = None, None
-    for _ in range(ITERS):
-        w = apply(v)
-        if last is not None:
-            w = [x - off * y for x, y in zip(w, last)]
-        middle = dot(v, w)
-        w = [x - middle * y for x, y in zip(w, v)]
-        last = v
-        off, v = unit(w)
-        entries += [middle, off]
-        basis.append(v)
+    def ratio(a, b):
+        return jnp.where(b > 0.0, a / jnp.where(b > 0.0, b, 1.0), 0.0)
 
     def put(row, value, which):
         for r in which:
             out_ref[pl.ds(r * sent_rows + row, groups, stride=reps * sent_rows), :] = value
 
-    for k, v in enumerate(basis):
-        for part, tiles in enumerate((turned(v, 2 + k), v)):
-            for half in range(groups // side):
-                row = jnp.zeros(tile, F32)
-                for q in range(side):
-                    row = jnp.where(segment == q, shifted(tiles[half * side + q], q - part), row)
-                put(2 * k + part, row, range(half, reps, HALVES))
+    def own_rows(rep):
+        return [of_groups(at_own + half, rep) for half in halves]
+
+    def owned(rep, slot):
+        return folded(turned(unfold(rep, 0), slot), 0)
+
+    weight = [of_groups(at_base, r) * jnp.exp(x) for r, x in enumerate(along(own_rows(0), owned(1, 0)))]
+    v = own_rows(2) + own_rows(3)
+    on_jobs = along(own_rows(2), owned(3, 1))
+    last = last_on_jobs = None
+    sizes, middles, scales, backs = [], [], [], []
+    for k in range(ITERS + 1):
+        if k:
+            q = [x * y for x, y in zip(weight, on_jobs)]
+            sizes.append(dot(v, v))
+            middles.append(ratio(dot(q, on_jobs), sizes[-1]))
+        tiles = scatter(q if k else weight, k)
+        rows_of_w = turned(tiles, 2 + k)
+        res = folded(rows_of_w, 0)
+        w = res + folded(tiles, 1)
+        w_on_jobs = along(res, folded(rows_of_w, 1))
+        if k:
+            square = dot(tiles, tiles)
+            scale = jnp.where(square > 0.0, lax.rsqrt(jnp.where(square > 0.0, square, 1.0)), 0.0)
+            if last is not None:
+                backs.append(ratio(scales[-1] * sizes[-1], sizes[-2]))
+            scales.append(square * scale)
+
+            def step(x, y, z):
+                out = x - middles[-1] * y
+                return scale * (out if z is None else out - backs[-1] * z)
+
+            nothing = [None] * max(len(v), reps)
+            following = [step(*t) for t in zip(w, v, last or nothing)]
+            following_on_jobs = [step(*t) for t in zip(w_on_jobs, on_jobs, last_on_jobs or nothing)]
+            last, last_on_jobs = v, on_jobs
+        else:
+            following = [y - x for x, y in zip(w, v)]
+            following_on_jobs = [y - x for x, y in zip(w_on_jobs, on_jobs)]
+        v, on_jobs = following, following_on_jobs
+        for part in range(2):
+            for half in halves:
+                put(2 * k + part, v[part * len(halves) + half], range(half, reps, HALVES))
     numbers = jnp.zeros(tile, F32)
-    for k, entry in enumerate(entries):
+    for k, entry in enumerate(sizes + middles + scales + backs):
         numbers = jnp.where(lane == k, entry, numbers)
     put(sent_rows - 1, numbers, range(reps))
     most = in_ref[pl.ds(at_head, groups * reps, stride=rows), :]
@@ -300,32 +325,34 @@
 
     numbers = take(sent_rows - 1)
     entry = lambda k: jnp.broadcast_to(numbers[:, k : k + 1], tile)
-    along = [entry(1 + 2 * k) for k in range(ITERS)]
-    off = [entry(2 + 2 * k) for k in range(ITERS)]
+    sizes, middles, scales, backs = ([entry(k * ITERS + j) for j in range(ITERS - (k == 3))] for k in range(4))
 
     def inner(a, b):
-        return jnp.sum(sum(x * y for x, y in zip(a, b)), axis=0, keepdims=True)
-
-    resid = [entry(0)]
-    direct = [entry(0)]
+        return jnp.sum(sum(g * (x * y) for g, x, y in zip(sizes, a, b)), axis=0, keepdims=True)
+
+    resid = [jnp.ones(tile, F32)]
+    direct = list(resid)
     step = []
     norm = inner(resid, resid)
     for turn in range(ITERS):
         image = []
         for k in range(turn + 2):
-            value = None
-            for term in ((off[k - 1], k - 1), (along[k] if k < ITERS else None, k), (off[k] if k < ITERS else None, k + 1)):
-                if 0 <= term[1] <= turn:
-                    product = term[0] * direct[term[1]]
-                    value = product if value is None else value + product
-            image.append(value)
+            terms = []
+            if k:
+                terms.append(scales[k - 1] * direct[k - 1])
+            if k <= turn:
+                terms.append((middles[k] + RIDGE) * direct[k])
+            if k < turn:
+                terms.append(backs[k] * direct[k + 1])
+            image.append(sum(terms))
         alpha = norm / inner(direct, image)
         step = [s + alpha * d for s, d in zip(step, direct)] + [alpha * d for d in direct[len(step) :]]
         resid = [r - alpha * i for r, i in zip(resid, image)] + [-alpha * i for i in image[len(resid) :]]
-        following = inner(resid, resid)
-        beta = following / norm
-        direct = [r + beta * d for r, d in zip(resid, direct)] + resid[len(direct) :]
-        norm = following
+        if turn + 1 < ITERS:
+            following = inner(resid, resid)
+            beta = following / norm
+            direct = [r + beta * d for r, d in zip(resid, direct)] + resid[len(direct) :]
+            norm = following
 
     for part in range(2):
         vectors = [take(2 * k + part) for k in range(ITERS + 1)]
@@ -406,10 +433,10 @@
         in_specs=[vmem],
         out_specs=(vmem, vmem),
         scratch_shapes=[
-            pltpu.VMEM((devices, 2 * groups, LANES), jnp.int32),
-            pltpu.VMEM((devices, 2 * groups, LANES), F32),
-            pltpu.VMEM((devices, groups, LANES), F32),
+            pltpu.VMEM((4, devices, LANES), F32),
+            pltpu.VMEM((groups, 2 * groups, reps * LANES), BF16),
             pltpu.VMEM((groups, 2 * BLK, reps * LANES), BF16),
+            pltpu.VMEM((ITERS + 1, 3, devices, LANES), F32),
             pltpu.VMEM((2 + ITERS + 1, groups * groups, LANES), F32),
         ],
         name="cell",

time: 32.8 us -> 32.3 us (0.985)
  Pallas kernels: 4.99 us -> 4.47 us
    pallas_call x1, Pallas kernels: 2.64 us -> 2.12 us  [owner_plan(): pl.pallas_call(functools.partial(cell_kernel, dims), out_shape=(pltpu.VME...]
where the time goes in v5:
time: 32.3 us; the launch traced here: 32.1 us
  blocking collectives  25 us (77%)
  Pallas kernels  4.47 us (14%)
  waiting for transfers between devices  0.99 us (3%)
  between operations  0.96 us (3%)
  starting transfers between devices  0.33 us (1%)
    all_to_all x1, blocking collectives, owner_plan(): lax.all_to_all(packed.reshape(devices, rows, 1, LANES), ALL, split_axis=0...  14.9 us
    all_to_all x1, blocking collectives, owner_plan(): lax.all_to_all(sent.reshape(devices, sent_rows, 1, LANES), ALL, split_axi...  10.1 us
    pallas_call x1, Pallas kernels, owner_plan(): pl.pallas_call(functools.partial(cell_kernel, dims), out_shape=(pltpu.VME...  2.12 us
    pallas_call x1, Pallas kernels, owner_plan(): pl.pallas_call(functools.partial(pack_kernel, dims), out_shape=pltpu.VMEM...  1.5 us
    ppermute x1, waiting for transfers between devices, owner_plan(): other = lax.ppermute(own, 'rep', [(r, r ^ 1) for r in range(reps)])  0.99 us
    pallas_call x1, Pallas kernels, owner_plan(): pl.pallas_call(functools.partial(place_kernel, dims), out_shape=(jax.Shap...  0.66 us
  transfers between devices with their start and end apart: 1, of which 1 were waited for; matrix products, arithmetic and copies ran while one was open for 0% of the time, Pallas kernels for 0%

profile of v5, /device:TPU:0, one launch (start us, length us, event | category | flops | bytes accessed | tf_op | source)
XLA Modules:
  0.0 32.1 jit_solution(8847097793769948331)
XLA Ops:
  0.6 1.5 %pack.1 = f32[192,128]{1,0:T(8,128)S(1)} custom-call(s32[8]{0:T(128)} %bitcast.130, f32[1,2048]{1,0:T(1,128)} %bitcast.125, s32[1,2048]{1,0:T(1,128)} %bitcast.122, s32[1,2048]{1,0:T(1,128)} %bitcast.123, s32[1,2048]{1,0:T(1,128)} %bitcast.124, f32[30,256]{1,0:T(8,128)} %a_ref.1, f32[30,256]{1,0:T(8,128)} %b_ref.1, f32[30,256]{1,0:T(8,128)} %c_ref.1, ...), custom_call_target="tpu_custom_call" | custom-call | tf_op jit(solution)/shard_map/pack/pallas_call | solution.py:415
  2.1 14.9 %all_to_all.41 = f32[32,6,1,128]{3,2,1,0:T(1,128)S(1)} all-to-all(f32[32,6,1,128]{3,2,1,0:T(1,128)S(1)} %bitcast.107), channel_id=1, replica_groups=mesh['geo'=8,'rep'=4] {'geo','rep'}, dimensions={0} | all-to-all | bytes 196608 | tf_op jit(solution)/shard_map/all_to_all | solution.py:426
  17.0 2.1 %cell.1 = (f32[288,128]{1,0:T(8,128)S(1)}, f32[1,128]{1,0:T(1,128)S(1)}) custom-call(f32[192,128]{1,0:T(8,128)S(1)} %bitcast.106), custom_call_target="tpu_custom_call" | custom-call | tf_op jit(solution)/shard_map/cell/pallas_call | solution.py:427
  19.2 10.1 %all_to_all.42 = f32[32,9,1,128]{3,2,1,0:T(1,128)S(1)} all-to-all(f32[32,9,1,128]{3,2,1,0:T(1,128)S(1)} %bitcast.108), channel_id=1, replica_groups=mesh['geo'=8,'rep'=4] {'geo','rep'}, dimensions={0} | all-to-all | bytes 294912 | tf_op jit(solution)/shard_map/all_to_all | solution.py:445
  29.3 0.0 copy-start.4
  29.3 0.0 copy-start.5
  29.3 0.0 copy-start.6
  29.3 0.0 copy-start.7
  29.4 0.2 join.1.own_ref
  29.6 0.0 copy-start
  29.6 0.0 copy-start.1
  29.6 0.0 copy-start.2
  29.6 0.0 copy-start.3
  29.6 0.3 %collective-permute-start = (f32[128,128]{1,0:T(8,128)S(1)}, f32[128,128]{1,0:T(8,128)S(1)}, u32[]{:S(2)}, u32[]{:S(2)}) collective-permute-start(f32[128,128]{1,0:T(8,128)S(1)} %join.1.own_ref), channel_id=1, source_target_pairs={{0,1},{1,0},{2,3},{3,2},{4,5},{5,4},{6,7},{7,6},{8,9},{9,8},{10,11... | collective-permute-start | bytes 196616 | tf_op jit(solution)/shard_map/ppermute | solution.py:453
  29.9 1.0 %collective-permute-done.other_ref = f32[128,128]{1,0:T(8,128)S(1)} collective-permute-done((f32[128,128]{1,0:T(8,128)S(1)}, f32[128,128]{1,0:T(8,128)S(1)}, u32[]{:S(2)}, u32[]{:S(2)}) %collective-permute-start) | collective-permute-done | bytes 65568 | tf_op jit(solution)/shard_map/ppermute | solution.py:453
  30.9 0.7 %place.1 = (f32[30,256]{1,0:T(8,128)}, f32[30,256]{1,0:T(8,128)}, f32[30,256]{1,0:T(8,128)}, f32[30,256]{1,0:T(8,128)}) custom-call(f32[128,128]{1,0:T(8,128)S(1)} %join.1.own_ref, f32[128,128]{1,0:T(8,128)S(1)} %collective-permute-done.other_ref), custom_call_target="tpu_custom_call" | custom-call | tf_op jit(solution)/shard_map/place/pallas_call | solution.py:454
  31.6 0.0 copy-done.4
  31.6 0.0 copy-done.5
  31.6 0.0 copy-done.6
  31.6 0.0 copy-done.7
  31.6 0.0 copy-done
  31.6 0.0 copy-done.1
  31.6 0.0 copy-done.2
  31.6 0.0 copy-done.3
  31.6 0.2 conditional.1
Async XLA Ops:
  29.3 2.2 %copy-start.4 = (s32[2048]{0:T(1024)S(1)}, s32[2048]{0:T(1024)}, u32[]{:S(2)}) copy-start(s32[2048]{0:T(1024)} %param.16) | copy-start | bytes 24580
  29.3 2.2 %copy-start.5 = (s32[2048]{0:T(1024)S(1)}, s32[2048]{0:T(1024)}, u32[]{:S(2)}) copy-start(s32[2048]{0:T(1024)} %param.17) | copy-start | bytes 24580
  29.3 2.2 %copy-start.6 = (s32[2048]{0:T(1024)S(1)}, s32[2048]{0:T(1024)}, u32[]{:S(2)}) copy-start(s32[2048]{0:T(1024)} %param.18) | copy-start | bytes 24580
  29.3 2.3 %copy-start.7 = (f32[2048]{0:T(1024)S(1)}, f32[2048]{0:T(1024)}, u32[]{:S(2)}) copy-start(f32[2048]{0:T(1024)} %param.15) | copy-start | bytes 24580
  29.6 2.0 %copy-start = (f32[30,256]{1,0:T(8,128)S(1)}, f32[30,256]{1,0:T(8,128)}, u32[]{:S(2)}) copy-start(f32[30,256]{1,0:T(8,128)} %b_ref.1) | copy-start | bytes 92164
  29.6 2.0 %copy-start.1 = (f32[30,256]{1,0:T(8,128)S(1)}, f32[30,256]{1,0:T(8,128)}, u32[]{:S(2)}) copy-start(f32[30,256]{1,0:T(8,128)} %a_ref.1) | copy-start | bytes 92164
  29.6 2.0 %copy-start.2 = (f32[30,256]{1,0:T(8,128)S(1)}, f32[30,256]{1,0:T(8,128)}, u32[]{:S(2)}) copy-start(f32[30,256]{1,0:T(8,128)} %c_ref.1) | copy-start | bytes 92164
  29.6 2.0 %copy-start.3 = (f32[30,256]{1,0:T(8,128)S(1)}, f32[30,256]{1,0:T(8,128)}, u32[]{:S(2)}) copy-start(f32[30,256]{1,0:T(8,128)} %d_ref.1) | copy-start | bytes 92164
  29.6 1.3 %collective-permute-start = (f32[128,128]{1,0:T(8,128)S(1)}, f32[128,128]{1,0:T(8,128)S(1)}, u32[]{:S(2)}, u32[]{:S(2)}) collective-permute-start(f32[128,128]{1,0:T(8,128)S(1)} %join.1.own_ref), channel_id=1, source_target_pairs={{0,1},{1,0},{2,3},{3,2},{4,5},{5,4},{6,7},{7,6},{8,9},{9,8},{10,11... | collective-permute-start | bytes 196616 | tf_op jit(solution)/shard_map/ppermute | solution.py:453

commit v6 on v5

--- a/solution.py
+++ b/solution.py
@@ -107,7 +107,11 @@
     chunk = 256
     cell = cell_ref[...]
     member = lax.broadcasted_iota(jnp.int32, (devices, jobs), 0) == cell
-    member_b = member.astype(F32).astype(BF16)
+    narrow = lambda x, n: jnp.broadcast_to(x.astype(F32), (n, jobs)).astype(BF16)
+    number = lambda n: lax.broadcasted_iota(jnp.int32, (n, jobs), 0).astype(F32).astype(BF16)
+    one, none = (lambda n: jnp.ones((n, jobs), BF16)), (lambda n: jnp.zeros((n, jobs), BF16))
+    member_n = number(devices) == narrow(cell, devices)
+    member_b = jnp.where(member_n, one(devices), none(devices))
     before = lax.broadcasted_iota(jnp.int32, (chunk, chunk), 0) < lax.broadcasted_iota(jnp.int32, (chunk, chunk), 1)
     before = before.astype(F32).astype(BF16)
     ranks = []
@@ -120,12 +124,17 @@
         count = count + jnp.sum(own.astype(F32), axis=1, keepdims=True)
     rank = jnp.concatenate(ranks, axis=1).astype(jnp.int32)
     largest = jnp.max(count, axis=0, keepdims=True)
-    chosen = (lax.broadcasted_iota(jnp.int32, (cap, jobs), 0) == rank).astype(F32).astype(BF16)
+    rank = jnp.where(rank < cap, rank, LANES)
+    chosen = jnp.where(number(LANES) == narrow(rank, LANES), one(LANES), none(LANES))
     values = (res_ref[...].astype(F32), slot_ref[...].astype(F32)) + tuple(x.astype(F32) for x in split3(base_ref[...]))
-    held = jnp.concatenate([jnp.where(member, value, 0.0).astype(BF16) for value in values], axis=0)
+    held = jnp.concatenate([jnp.where(member_n, narrow(value, devices), none(devices)) for value in values], axis=0)
     moved = dot_nt(held, chosen)
     moved = [moved[k * devices : (k + 1) * devices] for k in range(len(values))]
-    sent = (moved[0], moved[1], moved[2] + moved[3] + moved[4])
+    lane = lax.broadcasted_iota(jnp.int32, (devices, LANES), 1)
+    head = jnp.zeros((devices, LANES), F32)
+    for p in range(listed):
+        head = jnp.where(lane == cap + p, needed_ref[p].astype(F32), head)
+    sent = (moved[0] + head, jnp.where(lane < cap, moved[1], largest), moved[2] + moved[3] + moved[4])
 
     def put(row, value):
         out_ref[pl.ds(row, devices, stride=rows), :] = value
@@ -142,16 +151,11 @@
     for at in range(0, tracts, LANES):
         put(row, mine[:, at : at + LANES])
         row += 1
-    lane = lax.broadcasted_iota(jnp.int32, (devices, LANES), 1)
-    head = jnp.broadcast_to(largest, (devices, LANES))
-    for p in range(listed):
-        head = jnp.where(lane == p, needed_ref[p].astype(F32), head)
-    put(row, head)
 
 
 def cell_kernel(dims, in_ref, out_ref, flag_ref, digit_ref, mask_ref, hot_ref, part_ref, turn_ref):
-    rows, groups, reps, sent_rows = (dims[k] for k in ("rows", "groups", "reps", "sent_rows"))
-    at_res, at_slot, at_base, at_own, at_head = 0, 1, 2, 3, 5
+    rows, groups, reps, sent_rows, cap = (dims[k] for k in ("rows", "groups", "reps", "sent_rows", "cap"))
+    at_res, at_slot, at_base, at_own = 0, 1, 2, 3
     tile = (groups, LANES)
     side = LANES // BLK
     sub = lax.broadcasted_iota(jnp.int32, tile, 0)
@@ -176,13 +180,13 @@
             turn_ref[slot, pl.ds(b, groups, stride=groups), :] = x
         return [turn_ref[slot, pl.ds(g * groups, groups), :] for g in range(groups)]
 
-    head = of_groups(at_head, 0)
+    head = of_groups(at_res, 0)
     halves = range(groups // side)
-    choose = [jnp.take_along_axis(head, half * side + segment, axis=1).astype(jnp.int32) for half in halves]
+    choose = [jnp.take_along_axis(head, cap + half * side + segment, axis=1).astype(jnp.int32) for half in halves]
     need = []
     for g in range(groups):
-        row = jnp.broadcast_to(in_ref[pl.ds(g * reps * rows + at_head, 1), :], tile)
-        listed = jnp.sum(jnp.where(lane == sub, row, 0.0), axis=1, keepdims=True)
+        row = jnp.broadcast_to(in_ref[pl.ds(g * reps * rows + at_res, 1), :], tile)
+        listed = jnp.sum(jnp.where(lane == cap + sub, row, 0.0), axis=1, keepdims=True)
         need.append(jnp.where(segment == 1, listed, -1.0))
 
     tracts = [[of_groups(row, r).astype(jnp.int32) for r in range(reps)] for row in (at_res, at_slot)]
@@ -311,9 +315,8 @@
     for k, entry in enumerate(sizes + middles + scales + backs):
         numbers = jnp.where(lane == k, entry, numbers)
     put(sent_rows - 1, numbers, range(reps))
-    most = in_ref[pl.ds(at_head, groups * reps, stride=rows), :]
-    most = jnp.max(most, axis=0, keepdims=True)
-    flag_ref[...] = jnp.broadcast_to(most[:, LANES - 1 :], (1, LANES))
+    most = in_ref[pl.ds(at_slot, groups * reps, stride=rows), :]
+    flag_ref[0] = (jnp.max(most[:, cap:]) > float(cap)).astype(jnp.int32)
 
 
 def join_kernel(dims, in_ref, out_ref):
@@ -369,25 +372,21 @@
         out_ref[:, LANES:] = jnp.where(first, other, own)[:cells]
 
 
-def round_up(value, unit):
-    return -(-value // unit) * unit
-
-
 def plan_dims(mesh_shape, shapes):
     groups, reps = mesh_shape["geo"], mesh_shape["rep"]
     cells, tracts = shapes["lam"]
     listed = shapes["needed"][1] * shapes["needed"][2]
     slots = listed * BLK
     jobs = shapes["jobs"]
-    cap = round_up(max(1, 3 * jobs // (2 * cells)), LANES)
-    rows = 6
+    cap = LANES - listed
+    rows = 5
     fits = (
         groups * reps >= cells
         and reps == 4
         and groups == 8
         and listed == groups
         and tracts == groups * BLK == HALVES * LANES
-        and cap == LANES
+        and 3 * jobs <= 2 * cells * cap
         and jobs % 256 == 0
     )
     return fits, dict(
@@ -428,10 +427,10 @@
         functools.partial(cell_kernel, dims),
         out_shape=(
             pltpu.VMEM((devices * sent_rows, LANES), F32),
-            pltpu.VMEM((1, LANES), F32),
+            pltpu.SMEM((1,), jnp.int32),
         ),
         in_specs=[vmem],
-        out_specs=(vmem, vmem),
+        out_specs=(vmem, smem),
         scratch_shapes=[
             pltpu.VMEM((4, devices, LANES), F32),
             pltpu.VMEM((groups, 2 * groups, reps * LANES), BF16),
@@ -441,7 +440,7 @@
         ],
         name="cell",
     )(in_vmem(arrived.reshape(devices * rows, LANES)))
-    sent, over = lax.optimization_barrier((sent, (most[0, 0] > dims["cap"]).astype(jnp.int32)))
+    sent, over = lax.optimization_barrier((sent, most[0]))
     back = lax.all_to_all(sent.reshape(devices, sent_rows, 1, LANES), ALL, split_axis=0, concat_axis=0, tiled=True)
     own = pl.pallas_call(
         functools.partial(join_kernel, dims),
@@ -471,7 +470,7 @@
     outs, head, over, args = lax.optimization_barrier((outs, head, over, args[:4] + args[5:]))
 
     def other():
-        needed = head[dims["rows"] - 1, : dims["listed"]].astype(jnp.int32).reshape(shape)
+        needed = head[0, dims["cap"] :].astype(jnp.int32).reshape(shape)
         return tuple(start_plan(*args[:4], needed, *args[4:]))
 
     return lax.cond(over > 0, other, lambda: tuple(outs))

time: 32.3 us -> 32 us (level)
  no operation moved by 1% of the time
where the time goes in v6:
time: 32 us; the launch traced here: 31.8 us
  blocking collectives  24.8 us (78%)
  Pallas kernels  4.49 us (14%)
  waiting for transfers between devices  0.99 us (3%)
  between operations  0.9 us (3%)
  starting transfers between devices  0.33 us (1%)
    all_to_all x1, blocking collectives, owner_plan(): lax.all_to_all(packed.reshape(devices, rows, 1, LANES), ALL, split_axis=0...  14.7 us
    all_to_all x1, blocking collectives, owner_plan(): lax.all_to_all(sent.reshape(devices, sent_rows, 1, LANES), ALL, split_axi...  10.1 us
    pallas_call x1, Pallas kernels, owner_plan(): pl.pallas_call(functools.partial(cell_kernel, dims), out_shape=(pltpu.VME...  2.13 us
    pallas_call x1, Pallas kernels, owner_plan(): pl.pallas_call(functools.partial(pack_kernel, dims), out_shape=pltpu.VMEM...  1.5 us
    ppermute x1, waiting for transfers between devices, owner_plan(): other = lax.ppermute(own, 'rep', [(r, r ^ 1) for r in range(reps)])  0.99 us
    pallas_call x1, Pallas kernels, owner_plan(): pl.pallas_call(functools.partial(place_kernel, dims), out_shape=(jax.Shap...  0.66 us
  transfers between devices with their start and end apart: 1, of which 1 were waited for; matrix products, arithmetic and copies ran while one was open for 0% of the time, Pallas kernels for 0%

profile of v6, /device:TPU:0, one launch (start us, length us, event | category | flops | bytes accessed | tf_op | source)
XLA Modules:
  0.0 31.8 jit_solution(7597292529213793186)
XLA Ops:
  0.6 1.5 %pack.1 = f32[160,128]{1,0:T(8,128)S(1)} custom-call(s32[8]{0:T(128)} %bitcast.128, f32[1,2048]{1,0:T(1,128)} %bitcast.123, s32[1,2048]{1,0:T(1,128)} %bitcast.120, s32[1,2048]{1,0:T(1,128)} %bitcast.121, s32[1,2048]{1,0:T(1,128)} %bitcast.122, f32[30,256]{1,0:T(8,128)} %a_ref.1, f32[30,256]{1,0:T(8,128)} %b_ref.1, f32[30,256]{1,0:T(8,128)} %c_ref.1, ...), custom_call_target="tpu_custom_call" | custom-call | tf_op jit(solution)/shard_map/pack/pallas_call | solution.py:414
  2.1 14.7 %all_to_all.41 = f32[32,5,1,128]{3,2,1,0:T(1,128)S(1)} all-to-all(f32[32,5,1,128]{3,2,1,0:T(1,128)S(1)} %bitcast.106), channel_id=1, replica_groups=mesh['geo'=8,'rep'=4] {'geo','rep'}, dimensions={0} | all-to-all | bytes 163840 | tf_op jit(solution)/shard_map/all_to_all | solution.py:425
  16.8 2.1 %cell.1 = (f32[288,128]{1,0:T(8,128)S(1)}, s32[1]{0:T(128)S(4)}) custom-call(f32[160,128]{1,0:T(8,128)S(1)} %bitcast.105), custom_call_target="tpu_custom_call" | custom-call | tf_op jit(solution)/shard_map/cell/pallas_call | solution.py:426
  19.0 10.1 %all_to_all.42 = f32[32,9,1,128]{3,2,1,0:T(1,128)S(1)} all-to-all(f32[32,9,1,128]{3,2,1,0:T(1,128)S(1)} %bitcast.107), channel_id=1, replica_groups=mesh['geo'=8,'rep'=4] {'geo','rep'}, dimensions={0} | all-to-all | bytes 294912 | tf_op jit(solution)/shard_map/all_to_all | solution.py:444
  29.1 0.0 copy-start.4
  29.1 0.0 copy-start.5
  29.1 0.0 copy-start.6
  29.1 0.0 copy-start.7
  29.1 0.2 join.1.own_ref
  29.3 0.0 copy-start
  29.3 0.0 copy-start.1
  29.3 0.0 copy-start.2
  29.3 0.0 copy-start.3
  29.3 0.3 %collective-permute-start = (f32[128,128]{1,0:T(8,128)S(1)}, f32[128,128]{1,0:T(8,128)S(1)}, u32[]{:S(2)}, u32[]{:S(2)}) collective-permute-start(f32[128,128]{1,0:T(8,128)S(1)} %join.1.own_ref), channel_id=1, source_target_pairs={{0,1},{1,0},{2,3},{3,2},{4,5},{5,4},{6,7},{7,6},{8,9},{9,8},{10,11... | collective-permute-start | bytes 196616 | tf_op jit(solution)/shard_map/ppermute | solution.py:452
  29.7 1.0 %collective-permute-done.other_ref = f32[128,128]{1,0:T(8,128)S(1)} collective-permute-done((f32[128,128]{1,0:T(8,128)S(1)}, f32[128,128]{1,0:T(8,128)S(1)}, u32[]{:S(2)}, u32[]{:S(2)}) %collective-permute-start) | collective-permute-done | bytes 65568 | tf_op jit(solution)/shard_map/ppermute | solution.py:452
  30.7 0.7 %place.1 = (f32[30,256]{1,0:T(8,128)}, f32[30,256]{1,0:T(8,128)}, f32[30,256]{1,0:T(8,128)}, f32[30,256]{1,0:T(8,128)}) custom-call(f32[128,128]{1,0:T(8,128)S(1)} %join.1.own_ref, f32[128,128]{1,0:T(8,128)S(1)} %collective-permute-done.other_ref), custom_call_target="tpu_custom_call" | custom-call | tf_op jit(solution)/shard_map/place/pallas_call | solution.py:453
  31.3 0.0 copy-done.4
  31.3 0.0 copy-done.5
  31.3 0.0 copy-done.6
  31.3 0.0 copy-done.7
  31.3 0.0 copy-done
  31.4 0.0 copy-done.1
  31.4 0.0 copy-done.2
  31.4 0.0 copy-done.3
  31.4 0.2 conditional.1
Async XLA Ops:
  29.1 2.2 %copy-start.4 = (s32[2048]{0:T(1024)S(1)}, s32[2048]{0:T(1024)}, u32[]{:S(2)}) copy-start(s32[2048]{0:T(1024)} %param.16) | copy-start | bytes 24580
  29.1 2.2 %copy-start.5 = (s32[2048]{0:T(1024)S(1)}, s32[2048]{0:T(1024)}, u32[]{:S(2)}) copy-start(s32[2048]{0:T(1024)} %param.17) | copy-start | bytes 24580
  29.1 2.2 %copy-start.6 = (s32[2048]{0:T(1024)S(1)}, s32[2048]{0:T(1024)}, u32[]{:S(2)}) copy-start(s32[2048]{0:T(1024)} %param.18) | copy-start | bytes 24580
  29.1 2.3 %copy-start.7 = (f32[2048]{0:T(1024)S(1)}, f32[2048]{0:T(1024)}, u32[]{:S(2)}) copy-start(f32[2048]{0:T(1024)} %param.15) | copy-start | bytes 24580
  29.3 2.0 %copy-start = (f32[30,256]{1,0:T(8,128)S(1)}, f32[30,256]{1,0:T(8,128)}, u32[]{:S(2)}) copy-start(f32[30,256]{1,0:T(8,128)} %b_ref.1) | copy-start | bytes 92164
  29.3 2.0 %copy-start.1 = (f32[30,256]{1,0:T(8,128)S(1)}, f32[30,256]{1,0:T(8,128)}, u32[]{:S(2)}) copy-start(f32[30,256]{1,0:T(8,128)} %a_ref.1) | copy-start | bytes 92164
  29.3 2.0 %copy-start.2 = (f32[30,256]{1,0:T(8,128)S(1)}, f32[30,256]{1,0:T(8,128)}, u32[]{:S(2)}) copy-start(f32[30,256]{1,0:T(8,128)} %c_ref.1) | copy-start | bytes 92164
  29.3 2.0 %copy-start.3 = (f32[30,256]{1,0:T(8,128)S(1)}, f32[30,256]{1,0:T(8,128)}, u32[]{:S(2)}) copy-start(f32[30,256]{1,0:T(8,128)} %d_ref.1) | copy-start | bytes 92164
  29.3 1.3 %collective-permute-start = (f32[128,128]{1,0:T(8,128)S(1)}, f32[128,128]{1,0:T(8,128)S(1)}, u32[]{:S(2)}, u32[]{:S(2)}) collective-permute-start(f32[128,128]{1,0:T(8,128)S(1)} %join.1.own_ref), channel_id=1, source_target_pairs={{0,1},{1,0},{2,3},{3,2},{4,5},{5,4},{6,7},{7,6},{8,9},{9,8},{10,11... | collective-permute-start | bytes 196616 | tf_op jit(solution)/shard_map/ppermute | solution.py:452
